TPU v7x, 128 devices: a whole 4x4x4 slice. The times are simulated.
128 devices in a mesh: space: 8 (over x, core), chan: 16 (over z, y).
Axes of the slice: x: 4, y: 4, z: 4, core: 2. Of those that a mesh axis runs over, the one named last changes fastest.
Arguments:
- grid_in: bfloat16 [227, 131072], P(None, ('space', 'chan')), may hold values from -6 to 6
- grid_embed_w: bfloat16 [512, 227], replicated, may hold values from -0.375 to 0.375
- g2m_w: bfloat16 [512, 512], replicated, may hold values from -0.25 to 0.25
- pair_w: bfloat16 [4, 2, 512, 512], replicated, may hold values from -0.25 to 0.25
- second_w: bfloat16 [5, 512, 512], replicated, may hold values from -0.25 to 0.25
- first_b: float32 [6, 512], replicated, may hold values from -4 to 4
- norm_gain: float32 [5, 512], replicated, may hold values from 0.5 to 1.5
- geom_w: bfloat16 [3, 512, 4], replicated, may hold values from -3 to 3
- out_w: bfloat16 [227, 512], replicated, may hold values from -0.25 to 0.25
- out_b: float32 [227], replicated, may hold values from -4 to 4
- g2m_geom: bfloat16 [4, 196608], P(None, ('space', 'chan')), may hold values from -6 to 6
- mesh_geom: bfloat16 [4, 262144], P(None, ('space', 'chan')), may hold values from -6 to 6
- m2g_geom: bfloat16 [4, 393216], P(None, ('space', 'chan')), may hold values from -6 to 6
- g2m_send: int32 [196608], P(('space', 'chan')), may hold values from 0 to 131071, as said below
- g2m_recv: int32 [196608], P(('space', 'chan')), may hold values from 0 to 65535, as said below
- mesh_recv: int32 [262144], P(('space', 'chan')), may hold values from 0 to 65535, as said below
- mesh_slot: int32 [262144], P(('space', 'chan')), may hold values from 0 to 2047
- mesh_rows: int32 [16384, 16], P(('space', 'chan')), may hold values from 0 to 511
- m2g_send: int32 [393216], P(('space', 'chan')), may hold values from 0 to 65535, as said below
Outputs:
- prediction: float32 [227, 131072], P(None, ('space', 'chan'))
- mesh_state: bfloat16 [512, 65536], P(None, ('space', 'chan'))
Inputs may be any that keep to these rules, and one draw needn't show every extreme that they name: `g2m_send`: the edges of block d (1536 edges each) send from grid cells d * 1024 - 256 to (d + 1) * 1024 + 255, within the grid. `g2m_recv`: the edges of block d (1536 edges each) end at mesh nodes d * 512 to (d + 1) * 512 - 1. `mesh_recv`: the edges of block d (2048 edges each) end at mesh nodes d * 512 to (d + 1) * 512 - 1. `m2g_send`: for grid cell g in block d = g // 1024, the edges 3g to 3g + 2 send from mesh nodes d * 512 - 128 to (d + 1) * 512 + 127, within the mesh.
All inputs are finite; a program needn't handle non-finite values.
Results may differ from a plain program's by a relative error of at most 0.0095.
Values may be sent and summed in bfloat16 or wider, within the bound.
A program may use at most 128 MiB of HBM per device.

v0:
```python
import jax
import jax.numpy as jnp
from jax import lax
from jax.sharding import PartitionSpec as P

M_DEV = 512


eps = 1e-05


def extended_2(x, sides, width):
    edges = {}
    for axis, dim in sides:
        size, length = (lax.axis_size(axis), x.shape[dim])
        up = [(i, (i + 1) % size) for i in range(size - 1)]
        last = lax.slice_in_dim(x, length - width, length, axis=dim)
        leading = lax.slice_in_dim(x, 0, width, axis=dim)
        edges[dim] = (
            lax.ppermute(last, axis, up),
            lax.ppermute(leading, axis, [(b, a) for a, b in up]),
        )
    done = []
    for _, dim in sides:
        low, high = edges[dim]
        around = [(width, width) if d in done else (0, 0) for d in range(x.ndim)]
        x = jnp.concatenate([jnp.pad(low, around), x, jnp.pad(high, around)], axis=dim)
        done.append(dim)
    return x


def padded(block, sides, width):
    for axis, dim in sides:
        count = lax.axis_size(axis)
        forward = [(i, i + 1) for i in range(count - 1)]
        backward = [(target, source) for source, target in forward]
        low = lax.ppermute(
            lax.slice_in_dim(block, block.shape[dim] - width, None, axis=dim), axis, forward
        )
        high = lax.ppermute(lax.slice_in_dim(block, 0, width, axis=dim), axis, backward)
        block = jnp.concatenate([low, block, high], axis=dim)
    return block


def by_rows(values, weight):
    return lax.dot_general(
        values, weight, (((1,), (1,)), ((), ())), preferred_element_type=jnp.float32
    )


def by_columns(values, weight):
    return lax.dot_general(
        values, weight, (((0,), (1,)), ((), ())), preferred_element_type=jnp.float32
    )


def layer_norm(values, gain_rows):
    row_mean = jnp.mean(values, axis=1)
    row_var = jnp.mean(values * values, axis=1) - row_mean * row_mean
    return (values - row_mean[:, None]) * lax.rsqrt(row_var + eps)[:, None] * gain_rows[None, :]


def edge_block(pre_act, weight, gain_rows):
    hidden = jax.nn.silu(pre_act).astype(jnp.bfloat16)
    return layer_norm(by_rows(hidden, weight), gain_rows).astype(jnp.bfloat16)


def sum_to_nodes(message, receivers, node_count):
    one_hot = (receivers[:, None] == jnp.arange(node_count, dtype=jnp.int32)[None, :]).astype(
        jnp.bfloat16
    )
    return lax.dot_general(
        one_hot, message, (((0,), (0,)), ((), ())), preferred_element_type=jnp.float32
    )


def body(
    grid_in,
    grid_embed_w,
    g2m_w,
    pair_w,
    second_w,
    first_b,
    norm_gain,
    geom_w,
    out_w,
    out_b,
    g2m_geom,
    mesh_geom,
    m2g_geom,
    g2m_send,
    g2m_recv,
    mesh_recv,
    mesh_slot,
    mesh_rows,
    m2g_send,
):
    width = grid_embed_w.shape[0]
    grid_cells = grid_in.shape[1]
    position = lax.axis_index(("space", "chan"))
    grid_latent = edge_block(
        by_columns(grid_in, grid_embed_w) + first_b[0][None, :], second_w[0], norm_gain[0]
    )
    stacked = jnp.concatenate([g2m_w, pair_w[2, 1], pair_w[3, 0]], axis=0)
    grid_terms = by_rows(grid_latent, stacked)
    encode_send = grid_terms[:, :width].astype(jnp.bfloat16)
    decode_grid = grid_terms[:, width : 2 * width]
    output_grid = grid_terms[:, 2 * width :]
    grid_reach = grid_cells // 4
    extended = extended_2(encode_send, ((("space", "chan"), 0),), grid_reach)
    sender_local = g2m_send - position * grid_cells + grid_reach
    pre_act = (
        extended[sender_local].astype(jnp.float32)
        + by_columns(g2m_geom, geom_w[0])
        + first_b[1][None, :]
    )
    message = edge_block(pre_act, second_w[1], norm_gain[1])
    mesh_latent = sum_to_nodes(message, g2m_recv - position * M_DEV, M_DEV).astype(jnp.bfloat16)
    link_terms = by_rows(mesh_latent, jnp.concatenate([pair_w[0, 0], pair_w[0, 1]], axis=0))
    link_send = link_terms[:, :width].astype(jnp.bfloat16)
    link_recv = link_terms[:, width:]
    space_count = lax.axis_size("space")
    chan_count = lax.axis_size("chan")
    outgoing = link_send[mesh_rows.reshape(-1)].reshape(space_count * chan_count, -1, width)
    arrived = lax.all_to_all(
        outgoing, ("space", "chan"), split_axis=0, concat_axis=0, tiled=True
    ).reshape(-1, width)
    recv_local = mesh_recv - position * M_DEV
    pre_act = (
        arrived[mesh_slot].astype(jnp.float32)
        + link_recv[recv_local]
        + by_columns(mesh_geom, geom_w[1])
        + first_b[2][None, :]
    )
    message = edge_block(pre_act, second_w[2], norm_gain[2])
    aggregate = sum_to_nodes(message, recv_local, M_DEV).astype(jnp.bfloat16)
    node_pre = (
        by_rows(mesh_latent, pair_w[1, 0]) + by_rows(aggregate, pair_w[1, 1]) + first_b[3][None, :]
    )
    node_hidden = jax.nn.silu(node_pre).astype(jnp.bfloat16)
    state_rows = (
        mesh_latent.astype(jnp.float32)
        + layer_norm(by_rows(node_hidden, second_w[3]), norm_gain[3])
    ).astype(jnp.bfloat16)
    decode_send = by_rows(state_rows, pair_w[2, 0]).astype(jnp.bfloat16)
    mesh_reach = M_DEV // 4
    widened = padded(decode_send, ((("space", "chan"), 0),), mesh_reach)
    mesh_sender = m2g_send - position * M_DEV + mesh_reach
    expanded = jnp.broadcast_to(decode_grid[:, None, :], (grid_cells, 3, width)).reshape(
        3 * grid_cells, width
    )
    pre_act = (
        widened[mesh_sender].astype(jnp.float32)
        + expanded
        + by_columns(m2g_geom, geom_w[2])
        + first_b[4][None, :]
    )
    message = edge_block(pre_act, second_w[4], norm_gain[4])
    gathered = (
        message.astype(jnp.float32).reshape(grid_cells, 3, width).sum(axis=1).astype(jnp.bfloat16)
    )
    out_pre = output_grid + by_rows(gathered, pair_w[3, 1]) + first_b[5][None, :]
    out_hidden = jax.nn.silu(out_pre).astype(jnp.bfloat16)
    prediction = by_rows(out_w, out_hidden) + out_b[:, None]
    return (prediction, state_rows.T)


def solution(mesh):
    return jax.shard_map(
        body,
        mesh=mesh,
        in_specs=(
            P(None, ("space", "chan")),
            P(),
            P(),
            P(),
            P(),
            P(),
            P(),
            P(),
            P(),
            P(),
            P(None, ("space", "chan")),
            P(None, ("space", "chan")),
            P(None, ("space", "chan")),
            P(("space", "chan")),
            P(("space", "chan")),
            P(("space", "chan")),
            P(("space", "chan")),
            P(("space", "chan"), None),
            P(("space", "chan")),
        ),
        out_specs=(P(None, ("space", "chan")), P(None, ("space", "chan"))),
        check_vma=False,
    )
```

profile of v0, /device:TPU:1, one launch (start us, length us, event | category | flops | bytes accessed | tf_op | source)
XLA Modules:
  0.0 181.0 jit_solution(9135124601848056414)
XLA Ops:
  2.5 2.9 %slice_bitcast_fusion.1 = (bf16[512,512]{1,0:T(8,128)(2,1)}, bf16[512,512]{1,0:T(8,128)(2,1)}, bf16[512,512]{1,0:T(8,128)(2,1)}, bf16[512,512]{1,0:T(8,128)(2,1)}) fusion(bf16[4,2,512,512]{3,2,1,0:T(8,128)(2,1)} %param.22), kind=kLoop, calls=%fused_computation.90 | loop fusion | bytes 4194304 | tf_op jit(solution)/shard_map/squeeze | solution.py:119
  5.4 3.5 %fusion.100 = (f32[1024]{0:T(1024)S(1)}, f32[1024]{0:T(1024)S(1)}, f32[1024,512]{0,1:T(8,128)}) fusion(bf16[5,512,512]{2,1,0:T(8,128)(2,1)} %param.23, bf16[227,1024]{1,0:T(8,128)(2,1)S(1)} %copy-done, bf16[512,227]{0,1:T(8,128)(2,1)S(1)} %copy-done.14, f32[512]{0:T(512)S(1)} %bitcast.109), kind=kOutput, calls=%fused_computation.135 | convolution fusion | flops 779614208 | bytes 3329024 | tf_op jit(solution)/shard_map/dot_general | solution.py:46
  9.0 6.7 %fusion.106 = (bf16[1024,1536]{1,0:T(8,128)(2,1)S(1)}, f32[1024,1536]{1,0:T(8,128)}) fusion(bf16[512,512]{1,0:T(8,128)(2,1)} %get-tuple-element.20, bf16[512,512]{1,0:T(8,128)(2,1)} %get-tuple-element.21, bf16[512,512]{1,0:T(8,128)(2,1)} %param.21, f32[1024,512]{0,1:T(8,128)} %get-tuple-element.47, f32[512]{0:T(512)S(1)} %bitcast.99, ...), kind=kOutput, calls=%fused_computation.141 | convolution fusion | flops 1619001344 | bytes 13117440 | tf_op jit(solution)/shard_map/dot_general | solution.py:46
  16.5 4.0 %collective-permute-start = (bf16[256,512]{1,0:T(8,128)(2,1)}, bf16[256,512]{1,0:T(8,128)(2,1)S(1)}, u32[]{:S(2)}, u32[]{:S(2)}) collective-permute-start(bf16[256,512]{1,0:T(8,128)(2,1)} %get-tuple-element.22), channel_id=1, source_target_pairs={{0,1},{1,2},{2,3},{3,4},{4,5},{5,6},{6,7},{7,8},{8,9},{9,10},{10,1... | collective-permute-start | bytes 786440 | tf_op jit(solution)/shard_map/ppermute | solution.py:20
  20.6 7.4 %collective-permute-start.1 = (bf16[256,512]{1,0:T(8,128)(2,1)}, bf16[256,512]{1,0:T(8,128)(2,1)}, u32[]{:S(2)}, u32[]{:S(2)}) collective-permute-start(bf16[256,512]{1,0:T(8,128)(2,1)} %get-tuple-element.23), channel_id=1, source_target_pairs={{1,0},{2,1},{3,2},{4,3},{5,4},{6,5},{7,6},{8,7},{9,8},{10,9},{11,1... | collective-permute-start | bytes 786440 | tf_op jit(solution)/shard_map/ppermute | solution.py:21
  30.3 4.1 %collective-permute-done.1 = bf16[256,512]{1,0:T(8,128)(2,1)} collective-permute-done((bf16[256,512]{1,0:T(8,128)(2,1)}, bf16[256,512]{1,0:T(8,128)(2,1)}, u32[]{:S(2)}, u32[]{:S(2)}) %collective-permute-start.1) | collective-permute-done | bytes 262176 | tf_op jit(solution)/shard_map/ppermute | solution.py:21
  34.4 1.4 pad_maximum_fusion
  35.9 4.8 %gather_fusion = bf16[1536,512]{1,0:T(8,128)(2,1)S(1)} fusion(bf16[1536,512]{1,0:T(8,128)(2,1)S(1)} %pad_maximum_fusion, s32[2048]{0:T(1024)S(1)} %pad_clamp_fusion), kind=kCustom, calls=%fused_computation | custom fusion | bytes 3151872 | tf_op jit(solution)/shard_map/gather | solution.py:113
  40.7 4.5 %fusion.99 = (f32[1536]{0:T(1024)S(1)}, f32[1536]{0:T(1024)S(1)}, f32[1536,512]{0,1:T(8,128)}) fusion(bf16[5,512,512]{2,1,0:T(8,128)(2,1)} %param.23, bf16[1536,512]{1,0:T(8,128)(2,1)S(1)} %gather_fusion, f32[512]{0:T(512)S(1)} %bitcast.108, bf16[4,1536]{1,0:T(4,128)(2,1)S(1)} %copy-done.18, bf16[3,512,4]{1,2,0:T(4,128)(2,1)S(1)} %copy-done.19), kind=kOutput, calls=%fused_computation.134 | convolution fusion | flops 820245504 | bytes 5273600 | tf_op jit(solution)/shard_map/dot_general | solution.py:46
  45.2 3.4 %fusion.31 = bf16[512,512]{1,0:T(8,128)(2,1)S(1)} fusion(f32[1536,512]{0,1:T(8,128)} %get-tuple-element.50, f32[512]{0:T(512)S(1)} %bitcast.107, f32[1536]{0:T(1024)S(1)} %get-tuple-element.42, f32[1536]{0:T(1024)S(1)} %get-tuple-element.41, s32[1536]{0:T(1024)S(1)} %broadcast_subtract_fusion.1), kind=kOutput, calls=%fused_computation.51 | convolution fusion | flops 810287104 | bytes 3690496 | tf_op jit(solution)/shard_map/dot_general | solution.py:72
  50.2 1.3 copy-done.2
  51.6 9.2 %gather_fusion.1 = bf16[2048,512]{1,0:T(8,128)(2,1)} fusion(bf16[512,512]{1,0:T(8,128)(2,1)S(1)} %slice.232, s32[2048]{0:T(1024)S(1)} %broadcast_clamp_fusion), kind=kCustom, calls=%fused_computation.1 | custom fusion | bytes 4202496 | tf_op jit(solution)/shard_map/gather | solution.py:124
  60.8 9.5 %all-to-all-start = ((bf16[128,16,512]{2,1,0:T(8,128)(2,1)}), bf16[128,16,512]{2,1,0:T(8,128)(2,1)S(1)}, u32[]{:S(2)}, u32[]{:S(2)}) async-start(bf16[128,16,512]{2,1,0:T(8,128)(2,1)} %bitcast.96), calls=%async_computation | async-start | bytes 4194304 | tf_op jit(solution)/shard_map/all_to_all | solution.py:125
  70.3 3.1 %slice.166 = f32[1024,512]{1,0:T(8,128)} slice(f32[1024,1536]{1,0:T(8,128)} %get-tuple-element.49), slice={[0:1024], [512:1024]} | slice | bytes 4194304 | tf_op jit(solution)/shard_map/slice | solution.py:107
  73.4 6.2 %broadcast_in_dim.14 = f32[1024,3,512]{2,1,0:T(4,128)} broadcast(f32[1024,512]{1,0:T(8,128)} %slice.166), dimensions={0,2} | broadcast | bytes 8388608 | tf_op jit(solution)/shard_map/broadcast_in_dim | solution.py:149
  79.6 10.8 %reshape.117 = f32[3072,512]{1,0:T(8,128)} reshape(f32[1024,3,512]{2,1,0:T(4,128)} %broadcast_in_dim.14) | data formatting | bytes 12582912 | tf_op jit(solution)/shard_map/reshape | solution.py:149
  90.5 1.3 slice.163
  91.8 8.9 %gather_fusion.3 = f32[2048,512]{1,0:T(8,128)} fusion(f32[512,512]{1,0:T(8,128)S(1)} %slice.163, s32[2048]{0:T(1024)S(1)} %get-tuple-element.16), kind=kCustom, calls=%fused_computation.3 | custom fusion | bytes 8396800 | tf_op jit(solution)/shard_map/gather | solution.py:131
  100.6 2.7 %fusion.57 = f32[512,512]{1,0:T(8,128)} fusion(bf16[512,512]{1,0:T(8,128)(2,1)} %copy-done.3, bf16[4,2,512,512]{3,2,1,0:T(8,128)(2,1)} %param.22), kind=kOutput, calls=%fused_computation.77 | convolution fusion | flops 268435456 | bytes 2097152 | tf_op jit(solution)/shard_map/dot_general | solution.py:46
  103.3 9.2 %gather_fusion.2 = bf16[2048,512]{1,0:T(8,128)(2,1)} fusion(bf16[2048,512]{1,0:T(8,128)(2,1)S(1)} %bitcast.95, s32[2048]{0:T(1024)S(1)} %fusion.75), kind=kCustom, calls=%fused_computation.2 | custom fusion | bytes 4202496 | tf_op jit(solution)/shard_map/gather | solution.py:130
  112.5 7.3 %fusion.98 = (f32[2048]{0:T(1024)S(1)}, f32[2048]{0:T(1024)S(1)}, f32[2048,512]{0,1:T(8,128)}) fusion(bf16[5,512,512]{2,1,0:T(8,128)(2,1)} %param.23, f32[2048,512]{1,0:T(8,128)} %gather_fusion.3, bf16[2048,512]{1,0:T(8,128)(2,1)} %gather_fusion.2, bf16[4,2048]{1,0:T(4,128)(2,1)S(1)} %copy-done.17, f32[512]{0:T(512)S(1)} %bitcast.106, ...), kind=kOutput, calls=%fused_computation.133 | convolution fusion | flops 1094709248 | bytes 11048960 | tf_op jit(solution)/shard_map/dot_general | solution.py:46
  119.8 4.1 %fusion.34 = bf16[512,512]{1,0:T(8,128)(2,1)S(1)} fusion(f32[2048,512]{0,1:T(8,128)} %get-tuple-element.51, f32[512]{0:T(512)S(1)} %bitcast.105, f32[2048]{0:T(1024)S(1)} %get-tuple-element.40, f32[2048]{0:T(1024)S(1)} %get-tuple-element.39, s32[2048]{0:T(1024)S(1)} %get-tuple-element.17), kind=kOutput, calls=%fused_computation.53 | convolution fusion | flops 1080295424 | bytes 4745216 | tf_op jit(solution)/shard_map/dot_general | solution.py:72
  123.9 2.3 %fusion.101 = (f32[512]{0:T(512)S(1)}, f32[512]{0:T(512)S(1)}, f32[512,512]{0,1:T(8,128)S(1)}) fusion(bf16[5,512,512]{2,1,0:T(8,128)(2,1)} %param.23, f32[512,512]{1,0:T(8,128)S(1)} %copy-done.7, bf16[512,512]{1,0:T(8,128)(2,1)S(1)} %fusion.34, f32[512]{0:T(512)S(1)} %bitcast.104, bf16[4,2,512,512]{3,2,1,0:T(8,128)(2,1)} %param.22), kind=kOutput, calls=%fused_computation.136 | convolution fusion | flops 539491328 | bytes 3676160 | tf_op jit(solution)/shard_map/dot_general | solution.py:46
  126.8 1.5 convolution_convert_fusion
  128.4 3.3 %collective-permute-start.2 = (bf16[128,512]{1,0:T(8,128)(2,1)S(1)}, bf16[128,512]{1,0:T(8,128)(2,1)S(1)}, u32[]{:S(2)}, u32[]{:S(2)}) collective-permute-start(bf16[128,512]{1,0:T(8,128)(2,1)S(1)} %get-tuple-element.24), channel_id=1, source_target_pairs={{0,1},{1,2},{2,3},{3,4},{4,5},{5,6},{6,7},{7,8},{8,9},{9,10},{10,1... | collective-permute-start | bytes 393224 | tf_op jit(solution)/shard_map/ppermute | solution.py:37
  131.7 6.6 %collective-permute-start.3 = (bf16[128,512]{1,0:T(8,128)(2,1)S(1)}, bf16[128,512]{1,0:T(8,128)(2,1)S(1)}, u32[]{:S(2)}, u32[]{:S(2)}) collective-permute-start(bf16[128,512]{1,0:T(8,128)(2,1)S(1)} %get-tuple-element.25), channel_id=1, source_target_pairs={{1,0},{2,1},{3,2},{4,3},{5,4},{6,5},{7,6},{8,7},{9,8},{10,9},{11,1... | collective-permute-start | bytes 393224 | tf_op jit(solution)/shard_map/ppermute | solution.py:40
  140.0 13.2 %gather_fusion.4 = bf16[3072,512]{1,0:T(8,128)(2,1)} fusion(bf16[768,512]{1,0:T(8,128)(2,1)S(1)} %pad_maximum_fusion.1, s32[3072]{0:T(1024)S(1)} %fusion.74), kind=kCustom, calls=%fused_computation.4 | custom fusion | bytes 6303744 | tf_op jit(solution)/shard_map/gather | solution.py:153
  153.3 8.3 %fusion.97 = (f32[3072]{0:T(1024)S(1)}, f32[3072]{0:T(1024)S(1)}, f32[3072,512]{1,0:T(8,128)}) fusion(bf16[5,512,512]{2,1,0:T(8,128)(2,1)} %param.23, f32[3072,512]{1,0:T(8,128)} %reshape.117, bf16[3072,512]{1,0:T(8,128)(2,1)} %gather_fusion.4, f32[512]{0:T(512)S(1)} %bitcast.103, bf16[4,3072]{1,0:T(4,128)(2,1)S(1)} %copy-done.16, ...), kind=kOutput, calls=%fused_computation.132 | convolution fusion | flops 1642063872 | bytes 16308224 | tf_op jit(solution)/shard_map/dot_general | solution.py:46
  161.6 3.7 %multiply_convert_fusion = bf16[3072,512]{1,0:T(8,128)(2,1)S(1)} fusion(f32[3072,512]{1,0:T(8,128)} %get-tuple-element.53, f32[512]{0:T(512)S(1)} %bitcast.100, f32[3072]{0:T(1024)S(1)} %get-tuple-element.38, f32[3072]{0:T(1024)S(1)} %get-tuple-element.37), kind=kLoop, calls=%fused_computation.5 | loop fusion | flops 6291456 | bytes 9463808 | tf_op jit(solution)/shard_map/convert_element_type | solution.py:65
  165.3 4.3 %reshape.118 = bf16[1024,3,512]{2,1,0:T(4,128)(2,1)} reshape(bf16[3072,512]{1,0:T(8,128)(2,1)S(1)} %multiply_convert_fusion) | data formatting | bytes 6291456 | tf_op jit(solution)/shard_map/reshape | solution.py:160
  169.6 7.3 %reduce = bf16[1024,512]{1,0:T(8,128)(2,1)S(1)} reduce(bf16[1024,3,512]{2,1,0:T(4,128)(2,1)} %reshape.118, bf16[]{:T(256)} %constant.69), dimensions={1}, to_apply=%region_10.11.clone | reduce | flops 1048576 | bytes 4194306 | tf_op jit(solution)/shard_map/reduce_sum | solution.py:160
  176.9 4.1 %fusion.30 = f32[227,1024]{1,0:T(8,128)} fusion(bf16[227,512]{1,0:T(8,128)(2,1)S(1)} %copy-done.15, f32[1024,1536]{1,0:T(8,128)} %get-tuple-element.49, bf16[1024,512]{1,0:T(8,128)(2,1)S(1)} %reduce, f32[512]{0:T(512)S(1)} %bitcast.102, bf16[4,2,512,512]{3,2,1,0:T(8,128)(2,1)} %param.22, f32[227]{0:T(256)S(1)} %copy-done.20), kind=kOutput, calls=%fused_computation.50 | convolution fusion | flops 778800128 | bytes 4835212 | tf_op jit(solution)/shard_map/dot_general | solution.py:46
  (71 shorter events, 9.1 us)
Async XLA Ops:
  0.6 4.8 %copy-start = (bf16[227,1024]{1,0:T(8,128)(2,1)S(1)}, bf16[227,1024]{1,0:T(8,128)(2,1)}, u32[]{:S(2)}) copy-start(bf16[227,1024]{1,0:T(8,128)(2,1)} %param.19) | copy-start | bytes 1394692
  0.6 4.8 %copy-start.14 = (bf16[512,227]{0,1:T(8,128)(2,1)S(1)}, bf16[512,227]{0,1:T(8,128)(2,1)}, u32[]{:S(2)}) copy-start(bf16[512,227]{0,1:T(8,128)(2,1)} %param.20) | copy-start | bytes 697348
  9.0 19.0 %copy-start.9 = (s32[128,16]{0,1:T(8,128)S(1)}, s32[128,16]{0,1:T(8,128)}, u32[]{:S(2)}) copy-start(s32[128,16]{0,1:T(8,128)} %param.36) | copy-start | bytes 24580
  9.0 19.3 %copy-start.11 = (s32[1536]{0:T(1024)S(1)}, s32[1536]{0:T(1024)}, u32[]{:S(2)}) copy-start(s32[1536]{0:T(1024)} %param.32) | copy-start | bytes 18436
  15.7 13.6 %copy-start.12 = (s32[1536]{0:T(1024)S(1)}, s32[1536]{0:T(1024)}, u32[]{:S(2)}) copy-start(s32[1536]{0:T(1024)} %param.33) | copy-start | bytes 18436
  16.5 13.8 %collective-permute-start = (bf16[256,512]{1,0:T(8,128)(2,1)}, bf16[256,512]{1,0:T(8,128)(2,1)S(1)}, u32[]{:S(2)}, u32[]{:S(2)}) collective-permute-start(bf16[256,512]{1,0:T(8,128)(2,1)} %get-tuple-element.22), channel_id=1, source_target_pairs={{0,1},{1,2},{2,3},{3,4},{4,5},{5,6},{6,7},{7,8},{8,9},{9,10},{10,1... | collective-permute-start | bytes 786440 | tf_op jit(solution)/shard_map/ppermute | solution.py:20
  20.6 13.8 %collective-permute-start.1 = (bf16[256,512]{1,0:T(8,128)(2,1)}, bf16[256,512]{1,0:T(8,128)(2,1)}, u32[]{:S(2)}, u32[]{:S(2)}) collective-permute-start(bf16[256,512]{1,0:T(8,128)(2,1)} %get-tuple-element.23), channel_id=1, source_target_pairs={{1,0},{2,1},{3,2},{4,3},{5,4},{6,5},{7,6},{8,7},{9,8},{10,9},{11,1... | collective-permute-start | bytes 786440 | tf_op jit(solution)/shard_map/ppermute | solution.py:21
  35.8 4.8 %copy-start.18 = (bf16[4,1536]{1,0:T(4,128)(2,1)S(1)}, bf16[4,1536]{1,0:T(4,128)(2,1)}, u32[]{:S(2)}) copy-start(bf16[4,1536]{1,0:T(4,128)(2,1)} %param.29) | copy-start | bytes 36868
  35.8 4.8 %copy-start.19 = (bf16[3,512,4]{1,2,0:T(4,128)(2,1)S(1)}, bf16[3,512,4]{1,2,0:T(4,128)(2,1)}, u32[]{:S(2)}) copy-start(bf16[3,512,4]{1,2,0:T(4,128)(2,1)} %param.26) | copy-start | bytes 36868
  45.2 4.2 %copy-start.5 = (bf16[512,512]{1,0:T(8,128)(2,1)S(1)}, bf16[512,512]{1,0:T(8,128)(2,1)}, u32[]{:S(2)}) copy-start(bf16[512,512]{1,0:T(8,128)(2,1)} %get-tuple-element.18) | copy-start | bytes 1572868
  45.2 4.2 %copy-start.6 = (bf16[512,512]{1,0:T(8,128)(2,1)S(1)}, bf16[512,512]{1,0:T(8,128)(2,1)}, u32[]{:S(2)}) copy-start(bf16[512,512]{1,0:T(8,128)(2,1)} %get-tuple-element.19) | copy-start | bytes 1572868
  48.6 0.8 copy-start.3
  50.2 1.3 copy-start.2
  60.8 42.5 %all-to-all-start = ((bf16[128,16,512]{2,1,0:T(8,128)(2,1)}), bf16[128,16,512]{2,1,0:T(8,128)(2,1)S(1)}, u32[]{:S(2)}, u32[]{:S(2)}) async-start(bf16[128,16,512]{2,1,0:T(8,128)(2,1)} %bitcast.96), calls=%async_computation | async-start | bytes 4194304 | tf_op jit(solution)/shard_map/all_to_all | solution.py:125
  79.6 10.8 %copy-start.13 = (s32[2048]{0:T(1024)S(1)}, s32[2048]{0:T(1024)}, u32[]{:S(2)}) copy-start(s32[2048]{0:T(1024)} %param.35) | copy-start | bytes 24580
  79.6 10.8 %copy-start.10 = (s32[2048]{0:T(1024)S(1)}, s32[2048]{0:T(1024)}, u32[]{:S(2)}) copy-start(s32[2048]{0:T(1024)} %param.34) | copy-start | bytes 24580
  103.3 9.2 %copy-start.17 = (bf16[4,2048]{1,0:T(4,128)(2,1)S(1)}, bf16[4,2048]{1,0:T(4,128)(2,1)}, u32[]{:S(2)}) copy-start(bf16[4,2048]{1,0:T(4,128)(2,1)} %param.30) | copy-start | bytes 49156
  119.8 4.1 %copy-start.7 = (f32[512,512]{1,0:T(8,128)S(1)}, f32[512,512]{1,0:T(8,128)}, u32[]{:S(2)}) copy-start(f32[512,512]{1,0:T(8,128)} %fusion.57) | copy-start | bytes 3145732
  123.9 2.7 %copy-start.4 = (bf16[512,512]{1,0:T(8,128)(2,1)S(1)}, bf16[512,512]{1,0:T(8,128)(2,1)}, u32[]{:S(2)}) copy-start(bf16[512,512]{1,0:T(8,128)(2,1)} %copy-done.3) | copy-start | bytes 1572868
  126.2 12.1 %copy-start.8 = (s32[3072]{0:T(1024)S(1)}, s32[3072]{0:T(1024)}, u32[]{:S(2)}) copy-start(s32[3072]{0:T(1024)} %param.37) | copy-start | bytes 36868
  128.4 10.9 %collective-permute-start.2 = (bf16[128,512]{1,0:T(8,128)(2,1)S(1)}, bf16[128,512]{1,0:T(8,128)(2,1)S(1)}, u32[]{:S(2)}, u32[]{:S(2)}) collective-permute-start(bf16[128,512]{1,0:T(8,128)(2,1)S(1)} %get-tuple-element.24), channel_id=1, source_target_pairs={{0,1},{1,2},{2,3},{3,4},{4,5},{5,6},{6,7},{7,8},{8,9},{9,10},{10,1... | collective-permute-start | bytes 393224 | tf_op jit(solution)/shard_map/ppermute | solution.py:37
  131.7 8.3 %collective-permute-start.3 = (bf16[128,512]{1,0:T(8,128)(2,1)S(1)}, bf16[128,512]{1,0:T(8,128)(2,1)S(1)}, u32[]{:S(2)}, u32[]{:S(2)}) collective-permute-start(bf16[128,512]{1,0:T(8,128)(2,1)S(1)} %get-tuple-element.25), channel_id=1, source_target_pairs={{1,0},{2,1},{3,2},{4,3},{5,4},{6,5},{7,6},{8,7},{9,8},{10,9},{11,1... | collective-permute-start | bytes 393224 | tf_op jit(solution)/shard_map/ppermute | solution.py:40
  140.0 13.2 %copy-start.16 = (bf16[4,3072]{1,0:T(4,128)(2,1)S(1)}, bf16[4,3072]{1,0:T(4,128)(2,1)}, u32[]{:S(2)}) copy-start(bf16[4,3072]{1,0:T(4,128)(2,1)} %param.31) | copy-start | bytes 73732
  169.6 7.3 %copy-start.15 = (bf16[227,512]{1,0:T(8,128)(2,1)S(1)}, bf16[227,512]{1,0:T(8,128)(2,1)}, u32[]{:S(2)}) copy-start(bf16[227,512]{1,0:T(8,128)(2,1)} %param.27) | copy-start | bytes 697348
  169.6 7.3 %copy-start.20 = (f32[227]{0:T(256)S(1)}, f32[227]{0:T(256)}, u32[]{:S(2)}) copy-start(f32[227]{0:T(256)} %param.28) | copy-start | bytes 2728
  176.9 4.1 %copy-start.1 = (bf16[227,1024]{1,0:T(8,128)(2,1)S(1)}, bf16[227,1024]{1,0:T(8,128)(2,1)}, u32[]{:S(2)}) copy-start(bf16[227,1024]{1,0:T(8,128)(2,1)} %param.19) | copy-start | bytes 1394692
where the time goes:
time: 182 us; the launch traced here: 181 us
  local copies, waits for them, and re-layouts  81.5 us (45%)
  matrix products  49.1 us (27%)
  starting transfers between devices  30.8 us (17%)
  other arithmetic  12.8 us (7%)
  waiting for transfers between devices  5.76 us (3%)
    dot_general x10, matrix products, by_rows(): lax.dot_general(values, weight, (((1,), (1,)), ((), ())), preferred_eleme...  41.7 us
    gather x1, local copies, waits for them, and re-layouts, body(): widened[mesh_sender].astype(jnp.float32) + expanded  13.2 us
    reshape x1, local copies, waits for them, and re-layouts, body(): jnp.broadcast_to(decode_grid[:, None, :], (grid_cells, 3, width))  10.8 us
    all_to_all x1, starting transfers between devices, body(): lax.all_to_all(outgoing, ('space', 'chan'), split_axis=0, concat_axis=0,...  9.51 us
    gather x1, local copies, waits for them, and re-layouts, body(): link_send[mesh_rows.reshape(-1)]  9.17 us
    gather x1, local copies, waits for them, and re-layouts, body(): arrived[mesh_slot].astype(jnp.float32) + link_recv[recv_local]  9.17 us
    gather x1, local copies, waits for them, and re-layouts, body(): link_recv[recv_local]  8.88 us
    dot_general x2, matrix products, sum_to_nodes(): lax.dot_general(one_hot, message, (((0,), (0,)), ((), ())), preferred_ele...  7.45 us
  transfers between devices with their start and end apart: 5, of which 3 were waited for; matrix products, arithmetic and copies ran while one was open for 19% of the time, Pallas kernels for 0%

commit v1 on v0

v1 whole, which is shorter than its diff:
```python
import functools

import jax
import jax.numpy as jnp
from jax import lax
from jax.experimental import pallas as pl
from jax.experimental.pallas import tpu as pltpu
from jax.sharding import PartitionSpec as P

EPS = 1e-05
BF = jnp.bfloat16
F32 = jnp.float32
AXES = ("space", "chan")


def dot(a, b):
    return lax.dot_general(a, b, (((1,), (0,)), ((), ())), preferred_element_type=F32)


def dot_nt(a, b):
    return lax.dot_general(a, b, (((1,), (1,)), ((), ())), preferred_element_type=F32)


def dot_tn(a, b):
    return lax.dot_general(a, b, (((0,), (0,)), ((), ())), preferred_element_type=F32)


def silu(v):
    u = 0.5 * v
    return u + u * jnp.tanh(u)


def normed(y):
    n = y.shape[0]
    m = jnp.sum(y, axis=0, keepdims=True) * (1.0 / n)
    s = jnp.sum(y * y, axis=0, keepdims=True) * (1.0 / n)
    r = lax.rsqrt(s - m * m + EPS)
    return y * r - m * r


def one_hot(row, n):
    lanes = row.shape[1]
    return (lax.broadcasted_iota(jnp.int32, (n, lanes), 0) == row).astype(BF)


def columns_of(rows_ref, fb_ref, ng_ref, ob_ref=None):
    rows_ref[...] = jnp.zeros_like(rows_ref)
    rows_ref[0:6, :] = fb_ref[...]
    rows_ref[8:13, :] = ng_ref[...]
    if ob_ref is not None:
        rows_ref[16:17, 0 : ob_ref.shape[1]] = ob_ref[...]
    return rows_ref[...].T


def edge_columns(vec_ref, gwt_ref, bias):
    vec_ref[...] = jnp.zeros_like(vec_ref)
    vec_ref[0:4, :] = gwt_ref[0].astype(F32)
    for k in range(3):
        head = bias.astype(BF).astype(F32)
        vec_ref[4 + k : 5 + k, :] = head
        bias = bias - head
    return vec_ref[...].T.astype(BF)


def with_features(hot, feats):
    zeros = jnp.zeros((128 - feats.shape[0], feats.shape[1]), BF)
    return jnp.concatenate([hot, feats, zeros], axis=0)


def encode_kernel(
    cells,
    nodes,
    gin,
    we,
    w2a,
    g2m,
    w2b,
    p00,
    fb,
    ng,
    gw,
    geom,
    send,
    recv,
    rows,
    lat_out,
    ml_out,
    out_rows,
    vec,
    cols,
    sent,
    acc,
    embed,
):
    cols[...] = columns_of(vec, fb, ng)
    ext = gin.shape[1]
    embed[...] = jnp.zeros_like(embed)
    embed[:, 0 : we.shape[1]] = we[...]
    sent[:, ext:] = edge_columns(vec, gw, fb[1:2, :])
    halo = (ext - cells) // 2
    w = 256
    for i in range(ext // w):
        at = slice(i * w, (i + 1) * w)
        h = silu(dot(embed[...], gin[:, at]) + cols[:, 0:1]).astype(BF)
        lat = (normed(dot(w2a[0], h)) * cols[:, 8:9]).astype(BF)
        if halo <= i * w < halo + cells:
            lat_out[:, i * w - halo : (i + 1) * w - halo] = lat
        sent[:, at] = dot(g2m[...], lat).astype(BF)
    edges = send.shape[1]
    acc[...] = jnp.zeros_like(acc)
    for i in range(edges // w):
        at = slice(i * w, (i + 1) * w)
        pre = dot(sent[...], with_features(one_hot(send[:, at], ext), geom[:, at]))
        message = normed(dot(w2b[0], silu(pre).astype(BF))).astype(BF)
        acc[...] += dot_nt(message, one_hot(recv[:, at], nodes))
    ml = (acc[...] * cols[:, 9:10]).astype(BF)
    ml_out[...] = ml
    link = dot_nt(ml.astype(F32).T.astype(BF), p00[0, 0]).astype(BF)
    for i in range(rows.shape[1] // w):
        at = slice(i * w, (i + 1) * w)
        out_rows[at, :] = dot_tn(one_hot(rows[:, at], nodes), link).astype(BF)


def mesh_kernel(
    arrived,
    ml,
    p01,
    w2c,
    p10,
    p11,
    w2d,
    p20,
    fb,
    ng,
    gw,
    geom,
    slot,
    recv,
    state_out,
    ds_out,
    vec,
    cols,
    arr_t,
    acc,
):
    cols[...] = columns_of(vec, fb, ng)
    nodes = ml.shape[1]
    slots = arrived.shape[0]
    w = 256
    for i in range(slots // w):
        at = slice(i * w, (i + 1) * w)
        arr_t[:, at] = arrived[at, :].T
    link = dot(p01[0, 0], ml[...]).astype(BF)
    arr_t[:, slots:] = edge_columns(vec, gw, fb[2:3, :])
    acc[...] = jnp.zeros_like(acc)
    for i in range(slot.shape[1] // w):
        at = slice(i * w, (i + 1) * w)
        to = one_hot(recv[:, at], nodes)
        pre = (
            dot(arr_t[...], with_features(one_hot(slot[:, at], slots), geom[:, at]))
            + dot(link, to)
        )
        message = normed(dot(w2c[0], silu(pre).astype(BF))).astype(BF)
        acc[...] += dot_nt(message, to)
    aggregate = (acc[...] * cols[:, 10:11]).astype(BF)
    hidden = silu(dot(p10[0, 0], ml[...]) + dot(p11[0, 0], aggregate) + cols[:, 3:4]).astype(BF)
    state = (ml[...].astype(F32) + normed(dot(w2d[0], hidden)) * cols[:, 11:12]).astype(BF)
    state_out[...] = state
    ds_out[...] = dot(p20[0, 0], state).astype(BF)


def decode_kernel(
    ds,
    lat,
    p21,
    p30,
    p31,
    w2e,
    ow,
    fb,
    ng,
    ob,
    gw,
    geom,
    send,
    pred_out,
    vec,
    cols,
    sent,
):
    cols[...] = columns_of(vec, fb, ng, ob)
    cells = lat.shape[1]
    reach = ds.shape[1]
    outs = ow.shape[0]
    sent[:, 0:reach] = ds[...]
    sent[:, reach:] = edge_columns(vec, gw, fb[4:5, :])
    w = 256
    for i in range(cells // w):
        at = slice(i * w, (i + 1) * w)
        here = lat[:, at]
        base = dot(p21[0, 0], here)
        total = jnp.zeros_like(base)
        for j in range(3):
            hot = one_hot(send[j : j + 1, at], reach)
            pre = base + dot(sent[...], with_features(hot, geom[16 * j : 16 * j + 16, at]))
            message = normed(dot(w2e[0], silu(pre).astype(BF))).astype(BF)
            total += message.astype(F32)
        gathered = (total * cols[:, 12:13]).astype(BF)
        pre = dot(p30[0, 0], here) + dot(p31[0, 0], gathered) + cols[:, 5:6]
        pred_out[:, at] = dot(ow[...], silu(pre).astype(BF)) + cols[0:outs, 16:17]


def whole(x):
    nd = x.ndim
    return pl.BlockSpec(x.shape, lambda i: (0,) * nd)


def part(x, *index):
    nd = x.ndim
    lead = len(index)
    block = (1,) * lead + x.shape[lead:]
    full = tuple(index) + (0,) * (nd - lead)
    return pl.BlockSpec(block, lambda i: full)


def call(kernel, args, specs, outs, scratch, name):
    return pl.pallas_call(
        kernel,
        grid=(1,),
        in_specs=specs,
        out_specs=[whole(o) for o in outs],
        out_shape=outs,
        scratch_shapes=scratch,
        compiler_params=pltpu.CompilerParams(vmem_limit_bytes=56 << 20),
        name=name,
    )(*args)


def ends(x, width):
    n = lax.axis_size(AXES)
    forward = [(i, i + 1) for i in range(n - 1)]
    backward = [(b, a) for a, b in forward]
    low = lax.ppermute(x[:, x.shape[1] - width :], AXES, forward)
    high = lax.ppermute(x[:, :width], AXES, backward)
    return jnp.concatenate([low, x, high], axis=1)


def features(geom):
    return jnp.concatenate([geom, jnp.ones((3, geom.shape[1]), BF), jnp.zeros((9, geom.shape[1]), BF)])


def body(
    grid_in,
    grid_embed_w,
    g2m_w,
    pair_w,
    second_w,
    first_b,
    norm_gain,
    geom_w,
    out_w,
    out_b,
    g2m_geom,
    mesh_geom,
    m2g_geom,
    g2m_send,
    g2m_recv,
    mesh_recv,
    mesh_slot,
    mesh_rows,
    m2g_send,
):
    width = grid_embed_w.shape[0]
    cells = grid_in.shape[1]
    devices = mesh_rows.shape[0]
    nodes = 512
    position = lax.axis_index(AXES)
    shape = jax.ShapeDtypeStruct
    vec = pltpu.VMEM((128, width), F32)
    cols = pltpu.VMEM((width, 128), F32)

    reach = cells // 4
    gin = jnp.pad(ends(grid_in, reach), ((0, 256 - grid_in.shape[0]), (0, 0)))
    geom_wt = geom_w.transpose(0, 2, 1)
    send = (g2m_send - position * cells + reach).reshape(1, -1)
    recv = (g2m_recv - position * nodes).reshape(1, -1)
    rows = mesh_rows.reshape(1, -1)
    args = (gin, grid_embed_w, second_w, g2m_w, second_w, pair_w, first_b, norm_gain, geom_wt)
    geom = features(g2m_geom)
    args += (geom, send, recv, rows)
    specs = [
        whole(gin),
        whole(grid_embed_w),
        part(second_w, 0),
        whole(g2m_w),
        part(second_w, 1),
        part(pair_w, 0, 0),
        whole(first_b),
        whole(norm_gain),
        part(geom_wt, 0),
        whole(geom),
        whole(send),
        whole(recv),
        whole(rows),
    ]
    lat, ml, outgoing = call(
        functools.partial(encode_kernel, cells, nodes),
        args,
        specs,
        [shape((width, cells), BF), shape((width, nodes), BF), shape((rows.shape[1], width), BF)],
        [
            vec,
            cols,
            pltpu.VMEM((width, gin.shape[1] + 128), BF),
            pltpu.VMEM((width, nodes), F32),
            pltpu.VMEM((width, 256), BF),
        ],
        "encode",
    )

    arrived = lax.all_to_all(
        outgoing.reshape(devices, -1, width), AXES, split_axis=0, concat_axis=0, tiled=True
    ).reshape(-1, width)

    slot = mesh_slot.reshape(1, -1)
    recv = (mesh_recv - position * nodes).reshape(1, -1)
    args = (arrived, ml, pair_w, second_w, pair_w, pair_w, second_w, pair_w, first_b, norm_gain, geom_wt)
    geom = features(mesh_geom)
    args += (geom, slot, recv)
    specs = [
        whole(arrived),
        whole(ml),
        part(pair_w, 0, 1),
        part(second_w, 2),
        part(pair_w, 1, 0),
        part(pair_w, 1, 1),
        part(second_w, 3),
        part(pair_w, 2, 0),
        whole(first_b),
        whole(norm_gain),
        part(geom_wt, 1),
        whole(geom),
        whole(slot),
        whole(recv),
    ]
    state, ds = call(
        mesh_kernel,
        args,
        specs,
        [shape((width, nodes), BF), shape((width, nodes), BF)],
        [vec, cols, pltpu.VMEM((width, arrived.shape[0] + 128), BF), pltpu.VMEM((width, nodes), F32)],
        "mesh",
    )

    reach = nodes // 4
    ds = ends(ds, reach)
    send = (m2g_send - position * nodes + reach).reshape(cells, 3).T
    geom = features(m2g_geom).reshape(16, cells, 3).transpose(2, 0, 1).reshape(48, cells)
    ob = out_b.reshape(1, -1)
    args = (ds, lat, pair_w, pair_w, pair_w, second_w, out_w, first_b, norm_gain, ob, geom_wt, geom, send)
    specs = [
        whole(ds),
        whole(lat),
        part(pair_w, 2, 1),
        part(pair_w, 3, 0),
        part(pair_w, 3, 1),
        part(second_w, 4),
        whole(out_w),
        whole(first_b),
        whole(norm_gain),
        whole(ob),
        part(geom_wt, 2),
        whole(geom),
        whole(send),
    ]
    (prediction,) = call(
        decode_kernel,
        args,
        specs,
        [shape((out_w.shape[0], cells), F32)],
        [vec, cols, pltpu.VMEM((width, ds.shape[1] + 128), BF)],
        "decode",
    )
    return (prediction, state)


def solution(mesh):
    return jax.shard_map(
        body,
        mesh=mesh,
        in_specs=(
            P(None, AXES),
            P(),
            P(),
            P(),
            P(),
            P(),
            P(),
            P(),
            P(),
            P(),
            P(None, AXES),
            P(None, AXES),
            P(None, AXES),
            P(AXES),
            P(AXES),
            P(AXES),
            P(AXES),
            P(AXES, None),
            P(AXES),
        ),
        out_specs=(P(None, AXES), P(None, AXES)),
        check_vma=False,
    )
```

time: 182 us -> 131 us (0.72)
  local copies, waits for them, and re-layouts: 81.5 us -> 11.2 us
  Pallas kernels: 0 us -> 57.9 us
  matrix products: 49.1 us -> 0 us
  waiting for transfers between devices: 5.76 us -> 27.7 us
  other arithmetic: 12.8 us -> 6.09 us
  starting transfers between devices: 30.8 us -> 26.4 us
    pallas_call x0 -> x3, Pallas kernels: none -> 57.9 us  [call(): pl.pallas_call(kernel, grid=(1,), in_specs=specs, out_specs=[whole(o) for...]
    dot_general x12 -> x0, matrix products: 49.1 us -> none  [the longest x10 41.7 us: by_rows(): lax.dot_general(values, weight, (((1,), (1,)), ((), ())), preferred_eleme...]
    gather x5 -> x0, local copies, waits for them, and re-layouts: 45.3 us -> none  [the longest x1 13.2 us: body(): widened[mesh_sender].astype(jnp.float32) + expanded]
    all_to_all x1, waiting for transfers between devices: 0.01 us -> 27.7 us  [body(): lax.all_to_all(outgoing.reshape(devices, -1, width), AXES, split_axis=0,...]
    reshape x3 -> x6, local copies, waits for them, and re-layouts: 15.2 us -> 3.53 us  [the longest x2 1.13 us: body(): send = (m2g_send - position * nodes + reach).reshape(cells, 3).T]
    reduce_sum x1 -> x0, other arithmetic: 7.28 us -> none  [body(): message.astype(jnp.float32).reshape(grid_cells, 3, width).sum(axis=1)]
    broadcast_in_dim x1 -> x2, local copies, waits for them, and re-layouts: 6.25 us -> 0.01 us  [the longest x1 0.01 us: features(): jnp.ones((3, geom.shape[1]), BF)]
    slice x8 -> x2, local copies, waits for them, and re-layouts: 8.2 us -> 2.02 us  [ends(): low = lax.ppermute(x[:, x.shape[1] - width:], AXES, forward)]
  transfers between devices with their start and end apart: 5 -> 5, of which waited for: 3 -> 1; matrix products, arithmetic and copies ran while one was open for 19% -> 9% of each run, Pallas kernels for 0% -> 0%
where the time goes in v1:
time: 131 us; the launch traced here: 130 us
  Pallas kernels  57.9 us (44%)
  waiting for transfers between devices  27.7 us (21%)
  starting transfers between devices  26.4 us (20%)
  local copies, waits for them, and re-layouts  11.2 us (9%)
  other arithmetic  6.09 us (5%)
    pallas_call x3, Pallas kernels, call(): pl.pallas_call(kernel, grid=(1,), in_specs=specs, out_specs=[whole(o) for...  57.9 us
    all_to_all x1, waiting for transfers between devices, body(): lax.all_to_all(outgoing.reshape(devices, -1, width), AXES, split_axis=0,...  27.7 us
    ppermute x2, starting transfers between devices, ends(): high = lax.ppermute(x[:, :width], AXES, backward)  13.2 us
    ppermute x2, starting transfers between devices, ends(): low = lax.ppermute(x[:, x.shape[1] - width:], AXES, forward)  7.07 us
    all_to_all x1, starting transfers between devices, body(): lax.all_to_all(outgoing.reshape(devices, -1, width), AXES, split_axis=0,...  6.1 us
    unnamed x16, local copies, waits for them, and re-layouts  3.93 us
  transfers between devices with their start and end apart: 5, of which 1 were waited for; matrix products, arithmetic and copies ran while one was open for 9% of the time, Pallas kernels for 0%

profile of v1, /device:TPU:1, one launch (start us, length us, event | category | flops | bytes accessed | tf_op | source)
XLA Modules:
  0.0 130.0 jit_solution(4529913889603175506)
XLA Ops:
  0.6 1.0 fusion.6
  1.7 4.0 %collective-permute-start = (bf16[227,256]{1,0:T(8,128)(2,1)S(1)}, bf16[227,256]{1,0:T(8,128)(2,1)S(1)}, u32[]{:S(2)}, u32[]{:S(2)}) collective-permute-start(bf16[227,256]{1,0:T(8,128)(2,1)S(1)} %get-tuple-element.14), channel_id=1, source_target_pairs={{0,1},{1,2},{2,3},{3,4},{4,5},{5,6},{6,7},{7,8},{8,9},{9,10},{10,1... | collective-permute-start | bytes 348680 | tf_op jit(solution)/shard_map/ppermute | solution.py:243
  5.7 7.4 %collective-permute-start.1 = (bf16[227,256]{1,0:T(8,128)(2,1)S(1)}, bf16[227,256]{1,0:T(8,128)(2,1)S(1)}, u32[]{:S(2)}, u32[]{:S(2)}) collective-permute-start(bf16[227,256]{1,0:T(8,128)(2,1)S(1)} %get-tuple-element.15), channel_id=1, source_target_pairs={{1,0},{2,1},{3,2},{4,3},{5,4},{6,5},{7,6},{8,7},{9,8},{10,9},{11,1... | collective-permute-start | bytes 348680 | tf_op jit(solution)/shard_map/ppermute | solution.py:244
  13.1 0.7 broadcast_subtract_fusion.1
  13.8 0.6 reshape.38.recv
  14.4 0.1 pad.15.clone
  14.5 0.1 pad.16.clone
  14.6 1.4 %maximum_maximum_fusion.2.geom = bf16[16,1536]{1,0:T(8,128)(2,1)} fusion(bf16[4,1536]{1,0:T(4,128)(2,1)} %param.29, bf16[16]{0:T(256)(128)(2,1)S(1)} %pad.16.clone, bf16[16]{0:T(256)(128)(2,1)S(1)} %pad.15.clone), kind=kLoop, calls=%fused_computation.9 | loop fusion | flops 147456 | bytes 61504 | tf_op jit(solution)/shard_map/concatenate | solution.py:249
  16.0 0.7 subtract_add_fusion.1
  16.7 0.6 reshape.37.send
  17.3 1.8 %copy.29.we = bf16[512,227]{1,0:T(8,128)(2,1)} copy(bf16[512,227]{0,1:T(8,128)(2,1)} %param.20) | data formatting | bytes 464896 | tf_op args[1]
  19.1 0.8 copy.28
  19.9 0.7 reshape.39.rows
  20.6 0.9 fusion.4.gin
  21.5 18.1 %encode.1 = (bf16[512,1024]{1,0:T(8,128)(2,1)}, bf16[512,512]{1,0:T(8,128)(2,1)}, bf16[2048,512]{1,0:T(8,128)(2,1)}) custom-call(bf16[256,1536]{1,0:T(8,128)(2,1)} %fusion.4.gin, bf16[512,227]{1,0:T(8,128)(2,1)} %copy.29.we, bf16[5,512,512]{2,1,0:T(8,128)(2,1)} %w2e.1, bf16[512,512]{1,0:T(8,128)(2,1)} %g2m.1, bf16[5,512,512]{2,1,0:T(8,128)(2,1)} %w2e.1, ...), custom_call_target="tpu_custom_call" | custom-call | tf_op jit(solution)/shard_map/encode/pallas_call | solution.py:227
  39.7 6.1 %all-to-all-start = ((bf16[128,16,512]{2,1,0:T(8,128)(2,1)}), bf16[128,16,512]{2,1,0:T(8,128)(2,1)S(1)}, u32[]{:S(2)}, u32[]{:S(2)}) async-start(bf16[128,16,512]{2,1,0:T(8,128)(2,1)} %bitcast.13), calls=%async_computation | async-start | bytes 4194304 | tf_op jit(solution)/shard_map/all_to_all | solution.py:321
  45.8 0.6 broadcast_subtract_fusion
  46.4 0.7 maximum_maximum_fusion.1.geom
  47.1 0.1 maximum_maximum_fusion
  47.2 27.7 %all-to-all-done = bf16[128,16,512]{2,1,0:T(8,128)(2,1)S(1)} async-done(((bf16[128,16,512]{2,1,0:T(8,128)(2,1)}), bf16[128,16,512]{2,1,0:T(8,128)(2,1)S(1)}, u32[]{:S(2)}, u32[]{:S(2)}) %all-to-all-start) | async-done | bytes 2097184 | tf_op jit(solution)/shard_map/all_to_all | solution.py:321
  74.8 1.3 %copy-done = bf16[128,16,512]{2,1,0:T(8,128)(2,1)} copy-done((bf16[128,16,512]{2,1,0:T(8,128)(2,1)}, bf16[128,16,512]{2,1,0:T(8,128)(2,1)S(1)}, u32[]{:S(2)}) %copy-start) | copy-done | bytes 2097176
  76.2 21.6 %mesh.1 = (bf16[512,512]{1,0:T(8,128)(2,1)}, bf16[512,512]{1,0:T(8,128)(2,1)}) custom-call(bf16[2048,512]{1,0:T(8,128)(2,1)} %bitcast.11, bf16[512,512]{1,0:T(8,128)(2,1)} %get-tuple-element.8.ml, bf16[4,2,512,512]{3,2,1,0:T(8,128)(2,1)} %p31.1, bf16[5,512,512]{2,1,0:T(8,128)(2,1)} %w2e.1, bf16[4,2,512,512]{3,2,1,0:T(8,128)(2,1)} %p31.1, ...), custom_call_target="tpu_custom_call" | custom-call | tf_op jit(solution)/shard_map/mesh/pallas_call | solution.py:227
  97.8 1.0 fusion.5
  98.8 3.0 %collective-permute-start.2 = (bf16[512,128]{1,0:T(8,128)(2,1)S(1)}, bf16[512,128]{1,0:T(8,128)(2,1)S(1)}, u32[]{:S(2)}, u32[]{:S(2)}) collective-permute-start(bf16[512,128]{1,0:T(8,128)(2,1)S(1)} %get-tuple-element.12), channel_id=1, source_target_pairs={{0,1},{1,2},{2,3},{3,4},{4,5},{5,6},{6,7},{7,8},{8,9},{9,10},{10,1... | collective-permute-start | bytes 393224 | tf_op jit(solution)/shard_map/ppermute | solution.py:243
  101.8 5.8 %collective-permute-start.3 = (bf16[512,128]{1,0:T(8,128)(2,1)S(1)}, bf16[512,128]{1,0:T(8,128)(2,1)S(1)}, u32[]{:S(2)}, u32[]{:S(2)}) collective-permute-start(bf16[512,128]{1,0:T(8,128)(2,1)S(1)} %get-tuple-element.13), channel_id=1, source_target_pairs={{1,0},{2,1},{3,2},{4,3},{5,4},{6,5},{7,6},{8,7},{9,8},{10,9},{11,1... | collective-permute-start | bytes 393224 | tf_op jit(solution)/shard_map/ppermute | solution.py:244
  107.7 0.3 reshape.47
  108.0 0.8 copy.32
  108.8 0.4 copy.30
  109.2 0.5 reshape.45
  109.7 1.1 copy.31
  110.9 1.0 pad_maximum_fusion.ds
  111.9 18.1 %decode.1 = f32[227,1024]{1,0:T(8,128)} custom-call(bf16[512,768]{1,0:T(8,128)(2,1)} %pad_maximum_fusion.ds, bf16[512,1024]{1,0:T(8,128)(2,1)} %get-tuple-element.10.lat, bf16[4,2,512,512]{3,2,1,0:T(8,128)(2,1)} %p31.1, bf16[4,2,512,512]{3,2,1,0:T(8,128)(2,1)} %p31.1, bf16[4,2,512,512]{3,2,1,0:T(8,128)(2,1)} %p31.1, bf16[5,512,512]{2,1,0:T(8,128)(2,1)} %w2e.1, ...), custom_call_target="tpu_custom_call" | custom-call | tf_op jit(solution)/shard_map/decode/pallas_call | solution.py:227
  (20 shorter events, 0.1 us)
Async XLA Ops:
  0.6 19.9 %copy-start.2 = (bf16[227,1024]{1,0:T(8,128)(2,1)S(1)}, bf16[227,1024]{1,0:T(8,128)(2,1)}, u32[]{:S(2)}) copy-start(bf16[227,1024]{1,0:T(8,128)(2,1)} %param.19) | copy-start | bytes 1394692
  1.7 18.9 %collective-permute-start = (bf16[227,256]{1,0:T(8,128)(2,1)S(1)}, bf16[227,256]{1,0:T(8,128)(2,1)S(1)}, u32[]{:S(2)}, u32[]{:S(2)}) collective-permute-start(bf16[227,256]{1,0:T(8,128)(2,1)S(1)} %get-tuple-element.14), channel_id=1, source_target_pairs={{0,1},{1,2},{2,3},{3,4},{4,5},{5,6},{6,7},{7,8},{8,9},{9,10},{10,1... | collective-permute-start | bytes 348680 | tf_op jit(solution)/shard_map/ppermute | solution.py:243
  5.7 14.8 %collective-permute-start.1 = (bf16[227,256]{1,0:T(8,128)(2,1)S(1)}, bf16[227,256]{1,0:T(8,128)(2,1)S(1)}, u32[]{:S(2)}, u32[]{:S(2)}) collective-permute-start(bf16[227,256]{1,0:T(8,128)(2,1)S(1)} %get-tuple-element.15), channel_id=1, source_target_pairs={{1,0},{2,1},{3,2},{4,3},{5,4},{6,5},{7,6},{8,7},{9,8},{10,9},{11,1... | collective-permute-start | bytes 348680 | tf_op jit(solution)/shard_map/ppermute | solution.py:244
  39.6 6.1 %copy-start.6 = (s32[2048]{0:T(1024)S(1)}, s32[2048]{0:T(1024)}, u32[]{:S(2)}) copy-start(s32[2048]{0:T(1024)} %param.34) | copy-start | bytes 24580
  39.6 6.7 %copy-start.4 = (bf16[4,2048]{1,0:T(4,128)(2,1)S(1)}, bf16[4,2048]{1,0:T(4,128)(2,1)}, u32[]{:S(2)}) copy-start(bf16[4,2048]{1,0:T(4,128)(2,1)} %param.30) | copy-start | bytes 49156
  39.7 7.4 %copy-start.3 = (bf16[4,3072]{1,0:T(4,128)(2,1)S(1)}, bf16[4,3072]{1,0:T(4,128)(2,1)}, u32[]{:S(2)}) copy-start(bf16[4,3072]{1,0:T(4,128)(2,1)} %param.31) | copy-start | bytes 73732
  39.7 35.2 %all-to-all-start = ((bf16[128,16,512]{2,1,0:T(8,128)(2,1)}), bf16[128,16,512]{2,1,0:T(8,128)(2,1)S(1)}, u32[]{:S(2)}, u32[]{:S(2)}) async-start(bf16[128,16,512]{2,1,0:T(8,128)(2,1)} %bitcast.13), calls=%async_computation | async-start | bytes 4194304 | tf_op jit(solution)/shard_map/all_to_all | solution.py:321
  74.8 1.3 %copy-start = (bf16[128,16,512]{2,1,0:T(8,128)(2,1)}, bf16[128,16,512]{2,1,0:T(8,128)(2,1)S(1)}, u32[]{:S(2)}) copy-start(bf16[128,16,512]{2,1,0:T(8,128)(2,1)S(1)} %all-to-all-done) | copy-start | bytes 6291460
  76.2 31.5 %copy-start.5 = (s32[3072]{0:T(1024)S(1)}, s32[3072]{0:T(1024)}, u32[]{:S(2)}) copy-start(s32[3072]{0:T(1024)} %param.37) | copy-start | bytes 36868
  98.8 12.1 %collective-permute-start.2 = (bf16[512,128]{1,0:T(8,128)(2,1)S(1)}, bf16[512,128]{1,0:T(8,128)(2,1)S(1)}, u32[]{:S(2)}, u32[]{:S(2)}) collective-permute-start(bf16[512,128]{1,0:T(8,128)(2,1)S(1)} %get-tuple-element.12), channel_id=1, source_target_pairs={{0,1},{1,2},{2,3},{3,4},{4,5},{5,6},{6,7},{7,8},{8,9},{9,10},{10,1... | collective-permute-start | bytes 393224 | tf_op jit(solution)/shard_map/ppermute | solution.py:243
  101.8 9.1 %collective-permute-start.3 = (bf16[512,128]{1,0:T(8,128)(2,1)S(1)}, bf16[512,128]{1,0:T(8,128)(2,1)S(1)}, u32[]{:S(2)}, u32[]{:S(2)}) collective-permute-start(bf16[512,128]{1,0:T(8,128)(2,1)S(1)} %get-tuple-element.13), channel_id=1, source_target_pairs={{1,0},{2,1},{3,2},{4,3},{5,4},{6,5},{7,6},{8,7},{9,8},{10,9},{11,1... | collective-permute-start | bytes 393224 | tf_op jit(solution)/shard_map/ppermute | solution.py:244
  109.2 1.7 %copy-start.1 = (bf16[512,512]{1,0:T(8,128)(2,1)S(1)}, bf16[512,512]{1,0:T(8,128)(2,1)}, u32[]{:S(2)}) copy-start(bf16[512,512]{1,0:T(8,128)(2,1)} %get-tuple-element.9) | copy-start | bytes 1572868

commit v2 on v0

v2 whole, which is shorter than its diff:
```python
import functools

import jax
import jax.numpy as jnp
from jax import lax
from jax.experimental import pallas as pl
from jax.experimental.pallas import tpu as pltpu
from jax.sharding import PartitionSpec as P

EPS = 1e-05
BF = jnp.bfloat16
F32 = jnp.float32
AXES = ("space", "chan")
MESH = pl.DeviceIdType.MESH


def dot(a, b):
    return lax.dot_general(a, b, (((1,), (0,)), ((), ())), preferred_element_type=F32)


def dot_nt(a, b):
    return lax.dot_general(a, b, (((1,), (1,)), ((), ())), preferred_element_type=F32)


def dot_tn(a, b):
    return lax.dot_general(a, b, (((0,), (0,)), ((), ())), preferred_element_type=F32)


def silu(v):
    u = 0.5 * v
    return u + u * jnp.tanh(u)


def normed(y):
    n = y.shape[0]
    m = jnp.sum(y, axis=0, keepdims=True) * (1.0 / n)
    s = jnp.sum(y * y, axis=0, keepdims=True) * (1.0 / n)
    r = lax.rsqrt(s - m * m + EPS)
    return y * r - m * r


def one_hot(row, n):
    return (lax.broadcasted_iota(jnp.int32, (n, row.shape[1]), 0) == row).astype(BF)


def edge_columns(vec, gwt, bias):
    vec[...] = jnp.zeros_like(vec)
    vec[0:4, :] = gwt.astype(F32)
    for k in range(3):
        head = bias.astype(BF).astype(F32)
        vec[4 + k : 5 + k, :] = head
        bias = bias - head
    return vec[...].T.astype(BF)


def with_features(hot, feats):
    zeros = jnp.zeros((128 - feats.shape[0], feats.shape[1]), BF)
    return jnp.concatenate([hot, feats, zeros], axis=0)


def fill_features(ref, geom):
    ref[...] = jnp.zeros_like(ref)
    ref[0:4, :] = geom[...].astype(F32)
    ref[4:7, :] = jnp.ones((3, ref.shape[1]), F32)


def kernel(
    gin,
    wet,
    g2m,
    pair,
    second,
    fb,
    ng,
    gwt,
    ow,
    ob,
    geom1,
    geom2,
    geom3,
    send1,
    recv1,
    recv2,
    slot,
    rows_t,
    send3,
    pred_out,
    state_out,
    w_e,
    w_g,
    w_p,
    w_s,
    w_o,
    own,
    low,
    high,
    ginx,
    embed,
    vec,
    cols,
    feat1,
    feat2,
    feat3,
    feat4,
    sent,
    lat,
    base,
    outp,
    acc,
    ml,
    rows,
    outgoing,
    arrived,
    pre,
    ds,
    send4,
    w_sem,
    halo_send,
    halo_recv,
    a2a_send,
    a2a_recv,
    stage,
):
    s, c = lax.axis_index("space"), lax.axis_index("chan")
    me = s * 16 + c
    x, core, z, y = s // 2, s % 2, c // 4, c % 4
    cells, nodes = own.shape[1], ml.shape[1]
    reach1 = low.shape[1]
    reach3 = nodes // 4
    ext = cells + 2 * reach1
    width = ml.shape[0]

    def flat(d):
        d = (d + 128) % 128
        return (d // 16, d % 16)

    left, right = flat(me - 1), flat(me + 1)
    y_peers = [(s, z * 4 + (y + k) % 4) for k in (1, 2, 3)]
    z_peers = [(s, (z + k) % 4 * 4 + y) for k in (1, 2, 3)]
    x_peers = [((x + k) % 4 * 2 + core, c) for k in (1, 2, 3)]
    partners = [left, right, (x * 2 + 1 - core, c)] + y_peers + z_peers + x_peers
    barrier = pltpu.get_barrier_semaphore()
    for peer in partners:
        pl.semaphore_signal(barrier, inc=1, device_id=peer, device_id_type=MESH)

    def meet(k, peers):
        for peer in peers:
            pl.semaphore_signal(stage.at[k], inc=1, device_id=peer, device_id_type=MESH)

    copies = {}

    def fetch(name, src, dst):
        copies[name] = pltpu.make_async_copy(src, dst, w_sem.at[len(copies)])
        copies[name].start()

    fetch("own", gin, own)
    fetch("we", wet, w_e)
    fetch("s0", second.at[0], w_s.at[0])
    fetch("g2m", g2m, w_g)
    fetch("s1", second.at[1], w_s.at[1])
    fetch("p00", pair.at[0, 0], w_p.at[0, 0])
    fetch("p21", pair.at[2, 1], w_p.at[2, 1])
    fetch("p30", pair.at[3, 0], w_p.at[3, 0])
    fetch("p01", pair.at[0, 1], w_p.at[0, 1])
    fetch("s2", second.at[2], w_s.at[2])
    fetch("p10", pair.at[1, 0], w_p.at[1, 0])
    fetch("p11", pair.at[1, 1], w_p.at[1, 1])
    fetch("s3", second.at[3], w_s.at[3])
    fetch("p20", pair.at[2, 0], w_p.at[2, 0])
    fetch("s4", second.at[4], w_s.at[4])
    fetch("p31", pair.at[3, 1], w_p.at[3, 1])
    fetch("ow", ow, w_o)

    vec[...] = jnp.zeros_like(vec)
    vec[0:6, :] = fb[...]
    vec[8:13, :] = ng[...]
    vec[16:17, 0 : ob.shape[1]] = ob[...]
    cols[...] = vec[...].T
    embed[...] = jnp.zeros_like(embed)
    ginx[...] = jnp.zeros_like(ginx)
    sent[:, ext:] = edge_columns(vec, gwt[0], fb[1:2, :])
    fill_features(feat1, geom1)

    copies["own"].wait()
    copies["we"].wait()
    channels = own.shape[0]
    embed[0:channels, :] = w_e[...]

    pl.semaphore_wait(barrier, len(partners))
    to_right = pltpu.make_async_remote_copy(
        own.at[:, cells - reach1 :], low, halo_send.at[0], halo_recv.at[0], device_id=right, device_id_type=MESH
    )
    to_left = pltpu.make_async_remote_copy(
        own.at[:, 0:reach1], high, halo_send.at[1], halo_recv.at[1], device_id=left, device_id_type=MESH
    )
    to_right.start()
    to_left.start()
    meet(0, y_peers)

    def embedded(values):
        h = silu(dot_tn(embed[...], values) + cols[:, 0:1]).astype(BF)
        return (normed(dot(w_s[0], h)) * cols[:, 8:9]).astype(BF)

    ginx[0:channels, reach1 : reach1 + cells] = own[...]
    copies["s0"].wait()
    copies["g2m"].wait()
    lat[...] = embedded(ginx[:, reach1 : reach1 + cells])
    sent[:, reach1 : reach1 + cells] = dot(w_g[...], lat[...]).astype(BF)
    pl.semaphore_wait(stage.at[0], 3)
    meet(1, z_peers)

    spread = (
        lax.broadcasted_iota(jnp.int32, (128, rows.shape[1]), 0)
        == lax.broadcasted_iota(jnp.int32, (128, rows.shape[1]), 1) // 16
    ).astype(BF)
    lists = rows_t[...]
    picked = dot((lists // 16).astype(F32).astype(BF), spread) * 16.0 + dot(
        (lists % 16).astype(F32).astype(BF), spread
    )
    mine = (
        lax.broadcasted_iota(jnp.int32, picked.shape, 0)
        == lax.broadcasted_iota(jnp.int32, picked.shape, 1) % 16
    )
    rows[...] = jnp.sum(jnp.where(mine, picked, 0.0), axis=0, keepdims=True).astype(jnp.int32)

    to_right.wait()
    to_left.wait()
    ginx[0:channels, 0:reach1] = low[...]
    ginx[0:channels, reach1 + cells :] = high[...]
    ends = embedded(jnp.concatenate([ginx[:, 0:reach1], ginx[:, reach1 + cells :]], axis=1))
    ends = dot(w_g[...], ends).astype(BF)
    sent[:, 0:reach1] = ends[:, 0:reach1]
    sent[:, reach1 + cells : ext] = ends[:, reach1:]
    pl.semaphore_wait(stage.at[1], 3)
    meet(2, x_peers)

    w = 512
    acc[...] = jnp.zeros_like(acc)
    copies["s1"].wait()
    first1 = me * cells - reach1

    @pl.loop(0, send1.shape[0] // w)
    def _(i):
        at = pl.ds(pl.multiple_of(i * w, w), w)
        hot = one_hot(send1[at].reshape(1, w) - first1, ext)
        v = dot(sent[...], with_features(hot, feat1[:, at].astype(BF)))
        message = normed(dot(w_s[1], silu(v).astype(BF))).astype(BF)
        acc[...] += dot_nt(message, one_hot(recv1[at].reshape(1, w) - me * nodes, nodes))

    ml[...] = (acc[...] * cols[:, 9:10]).astype(BF)
    copies["p00"].wait()
    link = dot_nt(ml[...].astype(F32).T.astype(BF), w_p[0, 0]).astype(BF)
    pl.semaphore_wait(stage.at[2], 3)

    def out_copy(i, k):
        to_s, to_c = (s + i) % 8, (c + k) % 16
        to = to_s * 16 + to_c
        return pltpu.make_async_remote_copy(
            outgoing.at[pl.ds(to * 16, 16)],
            arrived.at[pl.ds(me * 16, 16)],
            a2a_send,
            a2a_recv.at[i],
            device_id=(to_s, to_c),
            device_id_type=MESH,
        )

    def make_rows(i):
        at = pl.ds(pl.multiple_of((s + i) % 8 * 256, 256), 256)
        outgoing[at, :] = dot_tn(one_hot(rows[:, at], nodes), link).astype(BF)

    @pl.loop(1, 8)
    def _(i):
        make_rows(i)

        @pl.loop(0, 16)
        def _(k):
            out_copy(i, k).start()

    make_rows(0)

    @pl.loop(1, 16)
    def _(k):
        out_copy(0, k).start()

    here = pl.ds(pl.multiple_of(me * 16, 16), 16)
    arrived[here, :] = outgoing[here, :]

    fill_features(feat2, geom2)
    fill_features(feat3, geom3)
    edges = pl.ds(0, w)
    copies["p01"].wait()
    own_link = jnp.concatenate(
        [dot(w_p[0, 1], ml[...]).astype(BF), edge_columns(vec, gwt[1], fb[2:3, :])], axis=1
    )

    @pl.loop(0, slot.shape[0] // w)
    def _(i):
        at = pl.ds(pl.multiple_of(i * w, w), w)
        hot = one_hot(recv2[at].reshape(1, w) - me * nodes, nodes)
        pre[:, at] = dot(own_link, with_features(hot, feat2[:, at].astype(BF)))

    copies["p21"].wait()
    copies["p30"].wait()
    base[...] = dot(w_p[2, 1], lat[...])
    outp[...] = dot(w_p[3, 0], lat[...]) + cols[:, 5:6]

    local = send3[...].reshape(1, 3 * cells) - (me * nodes - reach3)
    feat3[8:9, :] = (local // 16).astype(F32)
    feat3[9:10, :] = (local % 16).astype(F32)
    ds[:, nodes + 2 * reach3 :] = edge_columns(vec, gwt[2], fb[4:5, :])

    for q in range(cells // 256):
        part = feat3[:, q * 768 : (q + 1) * 768].astype(BF)
        for j in range(3):
            take = (
                lax.broadcasted_iota(jnp.int32, (768, 256), 0)
                == 3 * lax.broadcasted_iota(jnp.int32, (768, 256), 1) + j
            ).astype(BF)
            got = dot(part, take)
            at = (3 * (q // 2) + j) * w + q % 2 * 256
            feat4[:, at : at + 256] = got
            send4[:, at : at + 256] = (got[8:9, :] * 16.0 + got[9:10, :]).astype(jnp.int32)
    feat4[8:16, :] = jnp.zeros((8, feat4.shape[1]), F32)

    def take_rows(i, count):
        got = arrived.at[pl.ds(0, 16 * count)]
        pltpu.make_async_copy(got, got, a2a_recv.at[i]).wait()
        start = pl.multiple_of((s + 8 - i) % 8 * 256, 256)
        block = arrived[pl.ds(start, 256), :]

        @pl.loop(0, slot.shape[0] // w)
        def _(e):
            at = pl.ds(pl.multiple_of(e * w, w), w)
            pre[:, at] += dot_tn(block, one_hot(slot[at].reshape(1, w) - start, 256))

    @pl.loop(1, 8)
    def _(i):
        take_rows(i, 16)

    take_rows(0, 15)
    gone = outgoing.at[pl.ds(0, 16 * 127)]
    pltpu.make_async_copy(gone, gone, a2a_send).wait()

    acc[...] = jnp.zeros_like(acc)
    copies["s2"].wait()

    @pl.loop(0, slot.shape[0] // w)
    def _(i):
        at = pl.ds(pl.multiple_of(i * w, w), w)
        message = normed(dot(w_s[2], silu(pre[:, at]).astype(BF))).astype(BF)
        acc[...] += dot_nt(message, one_hot(recv2[at].reshape(1, w) - me * nodes, nodes))

    for name in ("p10", "p11", "s3", "p20"):
        copies[name].wait()

    def update(latent, total):
        aggregate = (total * cols[:, 10:11]).astype(BF)
        hidden = silu(dot(w_p[1, 0], latent) + dot(w_p[1, 1], aggregate) + cols[:, 3:4]).astype(BF)
        state = (latent.astype(F32) + normed(dot(w_s[3], hidden)) * cols[:, 11:12]).astype(BF)
        return state, dot(w_p[2, 0], state).astype(BF)

    last = nodes - reach3
    both = lambda ref: jnp.concatenate([ref[:, 0:reach3], ref[:, last:]], axis=1)
    state, out = update(both(ml), both(acc))
    state_out[:, 0:reach3] = state[:, 0:reach3]
    state_out[:, last:] = state[:, reach3:]
    ds[:, reach3 : 2 * reach3] = out[:, 0:reach3]
    ds[:, nodes : nodes + reach3] = out[:, reach3:]
    to_right = pltpu.make_async_remote_copy(
        ds.at[:, nodes : nodes + reach3],
        ds.at[:, 0:reach3],
        halo_send.at[2],
        halo_recv.at[2],
        device_id=right,
        device_id_type=MESH,
    )
    to_left = pltpu.make_async_remote_copy(
        ds.at[:, reach3 : 2 * reach3],
        ds.at[:, nodes + reach3 : nodes + 2 * reach3],
        halo_send.at[3],
        halo_recv.at[3],
        device_id=left,
        device_id_type=MESH,
    )
    to_right.start()
    to_left.start()
    state, out = update(ml[:, reach3:last], acc[:, reach3:last])
    state_out[:, reach3:last] = state
    ds[:, 2 * reach3 : nodes] = out
    for name in ("s4", "p31", "ow"):
        copies[name].wait()
    to_right.wait()
    to_left.wait()

    outs = ow.shape[0]

    @pl.loop(0, cells // w)
    def _(q):
        at = pl.ds(pl.multiple_of(q * w, w), w)
        total = jnp.zeros((width, w), F32)
        for j in range(3):
            edge = pl.ds(pl.multiple_of((3 * q + j) * w, w), w)
            hot = one_hot(send4[:, edge], nodes + 2 * reach3)
            v = base[:, at] + dot(ds[...], with_features(hot, feat4[:, edge].astype(BF)))
            total += normed(dot(w_s[4], silu(v).astype(BF))).astype(BF).astype(F32)
        gathered = (total * cols[:, 12:13]).astype(BF)
        hidden = silu(outp[:, at] + dot(w_p[3, 1], gathered)).astype(BF)
        pred_out[:, at] = dot(w_o[...], hidden) + cols[0:outs, 16:17]


def body(
    grid_in,
    grid_embed_w,
    g2m_w,
    pair_w,
    second_w,
    first_b,
    norm_gain,
    geom_w,
    out_w,
    out_b,
    g2m_geom,
    mesh_geom,
    m2g_geom,
    g2m_send,
    g2m_recv,
    mesh_recv,
    mesh_slot,
    mesh_rows,
    m2g_send,
):
    width, channels = grid_embed_w.shape
    cells = grid_in.shape[1]
    nodes = 512
    links = mesh_rows.size
    reach = cells // 4
    ext = cells + 2 * reach
    outs = out_w.shape[0]
    args = (
        grid_in,
        grid_embed_w.T,
        g2m_w,
        pair_w,
        second_w,
        first_b,
        norm_gain,
        geom_w.transpose(0, 2, 1),
        out_w,
        out_b.reshape(1, -1),
        g2m_geom,
        mesh_geom,
        m2g_geom,
        g2m_send,
        g2m_recv,
        mesh_recv,
        mesh_slot,
        mesh_rows.T,
        m2g_send,
    )
    hbm, vmem = pl.BlockSpec(memory_space=pl.ANY), pl.BlockSpec(memory_space=pltpu.VMEM)
    in_specs = [vmem] * len(args)
    for k in (0, 1, 2, 3, 4, 8):
        in_specs[k] = hbm
    V = pltpu.VMEM
    return tuple(
        pl.pallas_call(
            kernel,
            in_specs=in_specs,
            out_specs=[vmem, vmem],
            out_shape=[
                jax.ShapeDtypeStruct((outs, cells), F32),
                jax.ShapeDtypeStruct((width, nodes), BF),
            ],
            scratch_shapes=[
                V((channels, width), BF),
                V((width, width), BF),
                V(pair_w.shape, BF),
                V(second_w.shape, BF),
                V(out_w.shape, BF),
                V((channels, cells), BF),
                V((channels, reach), BF),
                V((channels, reach), BF),
                V((256, ext), BF),
                V((256, width), BF),
                V((128, width), F32),
                V((width, 128), F32),
                V((16, g2m_send.shape[0]), F32),
                V((16, mesh_slot.shape[0]), F32),
                V((16, m2g_send.shape[0]), F32),
                V((16, m2g_send.shape[0]), F32),
                V((width, ext + 128), BF),
                V((width, cells), BF),
                V((width, cells), F32),
                V((width, cells), F32),
                V((width, nodes), F32),
                V((width, nodes), BF),
                V((1, links), jnp.int32),
                V((links, width), BF),
                V((links, width), BF),
                V((width, mesh_slot.shape[0]), F32),
                V((width, nodes + nodes // 2 + 128), BF),
                V((1, m2g_send.shape[0]), jnp.int32),
                pltpu.SemaphoreType.DMA((17,)),
                pltpu.SemaphoreType.DMA((4,)),
                pltpu.SemaphoreType.DMA((4,)),
                pltpu.SemaphoreType.DMA,
                pltpu.SemaphoreType.DMA((8,)),
                pltpu.SemaphoreType.REGULAR((3,)),
            ],
            compiler_params=pltpu.CompilerParams(
                collective_id=0, has_side_effects=True, vmem_limit_bytes=60 << 20
            ),
            name="graph",
        )(*args)
    )


def solution(mesh):
    return jax.shard_map(
        body,
        mesh=mesh,
        in_specs=(
            P(None, AXES),
            P(),
            P(),
            P(),
            P(),
            P(),
            P(),
            P(),
            P(),
            P(),
            P(None, AXES),
            P(None, AXES),
            P(None, AXES),
            P(AXES),
            P(AXES),
            P(AXES),
            P(AXES),
            P(AXES, None),
            P(AXES),
        ),
        out_specs=(P(None, AXES), P(None, AXES)),
        check_vma=False,
    )
```

time: 182 us -> 82.6 us (0.45)
  the two profiles are of different devices: /device:TPU:1 before, /device:TPU:0 now
where the time goes in v2:
time: 82.6 us; the launch traced here: 82.3 us
  Pallas kernels  77.6 us (94%)
  local copies, waits for them, and re-layouts  4.09 us (5%)
    pallas_call x1, Pallas kernels, body(): pl.pallas_call(kernel, in_specs=in_specs, out_specs=[vmem, vmem], out_sha...  77.6 us
    unnamed x2, local copies, waits for them, and re-layouts  4.09 us

profile of v2, /device:TPU:0, one launch (start us, length us, event | category | flops | bytes accessed | tf_op | source)
XLA Modules:
  0.0 82.3 jit_solution(8265800053925068860)
XLA Ops:
  0.6 77.6 %graph.1 = (f32[227,1024]{1,0:T(8,128)}, bf16[512,512]{1,0:T(8,128)(2,1)}) custom-call(bf16[227,1024]{1,0:T(8,128)(2,1)} %gin.1, bf16[227,512]{1,0:T(8,128)(2,1)} %bitcast.4, bf16[512,512]{1,0:T(8,128)(2,1)} %g2m.1, bf16[4,2,512,512]{3,2,1,0:T(8,128)(2,1)} %pair.1, bf16[5,512,512]{2,1,0:T(8,128)(2,1)} %second.1, f32[6,512]{1,0:T(8,128)} %fb.1, f32[5,512]{1,0:T(8,128)} %ng.1, ...), custom_call_target="tpu_custom_call" | custom-call | tf_op jit(solution)/shard_map/graph/pallas_call | solution.py:466
  78.3 2.2 %copy.23 = f32[227,1024]{1,0:T(8,128)} copy(f32[227,1024]{1,0:T(8,128)} %get-tuple-element.4) | data formatting | bytes 1859584
  80.5 1.9 %copy.24 = bf16[512,512]{1,0:T(8,128)(2,1)} copy(bf16[512,512]{1,0:T(8,128)(2,1)} %get-tuple-element.5) | data formatting | bytes 1048576

commit v3 on v2

v3 whole, which is shorter than its diff:
```python
import functools

import jax
import jax.numpy as jnp
from jax import lax
from jax.experimental import pallas as pl
from jax.experimental.pallas import tpu as pltpu
from jax.sharding import PartitionSpec as P

EPS = 1e-05
BF = jnp.bfloat16
F32 = jnp.float32
AXES = ("space", "chan")
MESH = pl.DeviceIdType.MESH


def dot(a, b):
    return lax.dot_general(a, b, (((1,), (0,)), ((), ())), preferred_element_type=F32)


def dot_nt(a, b):
    return lax.dot_general(a, b, (((1,), (1,)), ((), ())), preferred_element_type=F32)


def dot_tn(a, b):
    return lax.dot_general(a, b, (((0,), (0,)), ((), ())), preferred_element_type=F32)


def silu(v):
    u = 0.5 * v
    return u + u * jnp.tanh(u)


def normed(y):
    n = y.shape[0]
    m = jnp.sum(y, axis=0, keepdims=True) * (1.0 / n)
    s = jnp.sum(y * y, axis=0, keepdims=True) * (1.0 / n)
    r = lax.rsqrt(s - m * m + EPS)
    return y * r - m * r


def one_hot(row, n):
    return (lax.broadcasted_iota(jnp.int32, (n, row.shape[1]), 0) == row).astype(BF)


def edge_columns(vec, gwt, bias):
    vec[...] = jnp.zeros_like(vec)
    vec[0:4, :] = gwt.astype(F32)
    for k in range(3):
        head = bias.astype(BF).astype(F32)
        vec[4 + k : 5 + k, :] = head
        bias = bias - head
    return vec[...].T.astype(BF)


def features(geom, extra=()):
    n = geom.shape[1]
    rows = [geom.astype(F32), jnp.ones((3, n), F32), jnp.zeros((1, n), F32)]
    return jnp.concatenate(rows + list(extra) + [jnp.zeros((8 - len(extra), n), F32)], axis=0)


def padded(feats):
    return jnp.concatenate([feats, jnp.zeros((256 - feats.shape[0], feats.shape[1]), F32)], axis=0).astype(BF)


def kernel(
    gin,
    wet,
    g2m,
    pair,
    second,
    fb,
    ng,
    gwt,
    ow,
    ob,
    geom1,
    geom2,
    geom3,
    send1,
    recv1,
    recv2,
    slot,
    rows_t,
    send3,
    pred_hbm,
    state_hbm,
    w_e,
    w_g,
    w_p,
    w_s,
    w_o,
    own,
    low,
    high,
    ginx,
    embed,
    vec,
    cols,
    feat,
    sent,
    lat,
    outp,
    acc,
    ml,
    outgoing,
    arrived,
    pre,
    pre3,
    ds,
    send4,
    pred_out,
    state_out,
    w_sem,
    halo_send,
    halo_recv,
    a2a_send,
    a2a_recv,
    out_sem,
    stage,
):
    s, c = lax.axis_index("space"), lax.axis_index("chan")
    me = s * 16 + c
    x, core, z, y = s // 2, s % 2, c // 4, c % 4
    cells, nodes = own.shape[1], ml.shape[1]
    reach1 = low.shape[1]
    reach3 = nodes // 4
    ext = cells + 2 * reach1
    width, links = ml.shape[0], arrived.shape[0]
    near3 = nodes + 2 * reach3

    def flat(d):
        d = (d + 128) % 128
        return (d // 16, d % 16)

    left, right = flat(me - 1), flat(me + 1)
    y_peers = [(s, z * 4 + (y + k) % 4) for k in (1, 2, 3)]
    z_peers = [(s, (z + k) % 4 * 4 + y) for k in (1, 2, 3)]
    x_peers = [((x + k) % 4 * 2 + core, c) for k in (1, 2, 3)]
    partners = [left, right, (x * 2 + 1 - core, c)] + y_peers + z_peers + x_peers
    barrier = pltpu.get_barrier_semaphore()
    for peer in partners:
        pl.semaphore_signal(barrier, inc=1, device_id=peer, device_id_type=MESH)

    def meet(k, peers):
        for peer in peers:
            pl.semaphore_signal(stage.at[k], inc=1, device_id=peer, device_id_type=MESH)

    copies = {}

    def fetch(name, src, dst):
        copies[name] = pltpu.make_async_copy(src, dst, w_sem.at[len(copies)])
        copies[name].start()

    fetch("own", gin, own)
    fetch("we", wet, w_e)
    fetch("s0", second.at[0], w_s.at[0])
    fetch("g2m", g2m, w_g)
    fetch("s1", second.at[1], w_s.at[1])
    fetch("p00", pair.at[0, 0], w_p.at[0, 0])
    fetch("p01", pair.at[0, 1], w_p.at[0, 1])
    fetch("p21", pair.at[2, 1], w_p.at[2, 1])
    fetch("p30", pair.at[3, 0], w_p.at[3, 0])
    fetch("s2", second.at[2], w_s.at[2])
    fetch("p10", pair.at[1, 0], w_p.at[1, 0])
    fetch("p11", pair.at[1, 1], w_p.at[1, 1])
    fetch("s3", second.at[3], w_s.at[3])
    fetch("p20", pair.at[2, 0], w_p.at[2, 0])
    fetch("s4", second.at[4], w_s.at[4])
    fetch("p31", pair.at[3, 1], w_p.at[3, 1])
    fetch("ow", ow, w_o)

    pl.semaphore_wait(barrier, len(partners))
    to_right = pltpu.make_async_remote_copy(
        gin.at[:, cells - reach1 :], low, halo_send.at[0], halo_recv.at[0], device_id=right, device_id_type=MESH
    )
    to_left = pltpu.make_async_remote_copy(
        gin.at[:, 0:reach1], high, halo_send.at[1], halo_recv.at[1], device_id=left, device_id_type=MESH
    )
    to_right.start()
    to_left.start()
    meet(0, y_peers)

    vec[...] = jnp.zeros_like(vec)
    vec[0:6, :] = fb[...]
    vec[8:13, :] = ng[...]
    vec[16:17, 0 : ob.shape[1]] = ob[...]
    cols[...] = vec[0:128, :].T
    embed[...] = jnp.zeros_like(embed)
    ginx[...] = jnp.zeros_like(ginx)
    sent[:, ext:] = edge_columns(vec, gwt[0], fb[1:2, :])

    copies["we"].wait()
    copies["own"].wait()
    channels = own.shape[0]
    embed[0:channels, :] = w_e[...]

    def embedded(values):
        h = silu(dot_tn(embed[...], values) + cols[:, 0:1]).astype(BF)
        return (normed(dot(w_s[0], h)) * cols[:, 8:9]).astype(BF)

    ginx[0:channels, 0:cells] = own[...]
    copies["s0"].wait()
    copies["g2m"].wait()
    lat[...] = embedded(ginx[:, 0:cells])
    sent[:, 0:cells] = dot(w_g[...], lat[...]).astype(BF)
    pl.semaphore_wait(stage.at[0], 3)
    meet(1, z_peers)

    w = 512
    edges1, edges2 = send1.shape[0], slot.shape[0]
    steps1 = [slice(i * w, (i + 1) * w) for i in range(edges1 // w)]
    steps2 = [slice(i * w, (i + 1) * w) for i in range(edges2 // w)]

    def sender(at):
        v = send1[at].reshape(1, w) - me * cells
        return jnp.where(v < 0, v + ext, v)

    for at in steps1:
        hot = one_hot(sender(at), cells)
        pre3[:, at] = dot(sent[:, 0:cells], hot) + dot(sent[:, ext:], padded(features(geom1[:, at])))

    r = lax.broadcasted_iota(jnp.int32, (1, links), 1) // 16
    dz, dy = r // 4 % 4, r % 4
    dx, dc = (r // 32 + dz + dy) % 4, r // 16 % 2
    to = ((x + dx) % 4 * 2 + (core + dc) % 2) * 16 + (z + dz) % 4 * 4 + (y + dy) % 4
    spread = (lax.broadcasted_iota(jnp.int32, (256, links), 0) == to).astype(BF)
    lists = jnp.concatenate([rows_t[...], jnp.zeros_like(rows_t)], axis=1)
    picked = dot((lists // 16).astype(F32).astype(BF), spread) * 16.0 + dot(
        (lists % 16).astype(F32).astype(BF), spread
    )
    mine = (
        lax.broadcasted_iota(jnp.int32, picked.shape, 0)
        == lax.broadcasted_iota(jnp.int32, picked.shape, 1) % 16
    )
    rows = jnp.sum(jnp.where(mine, picked, 0.0), axis=0, keepdims=True).astype(jnp.int32)

    to_right.wait()
    to_left.wait()
    ginx[0:channels, cells : cells + reach1] = high[...]
    ginx[0:channels, cells + reach1 :] = low[...]
    sent[:, cells:ext] = dot(w_g[...], embedded(ginx[:, cells:])).astype(BF)
    pl.semaphore_wait(stage.at[1], 3)
    meet(2, x_peers)

    copies["s1"].wait()

    def second_layer(k, v):
        return dot(w_s[k], silu(v).astype(BF))

    def pipelined(steps, make, use):
        held = None
        for i in range(len(steps) + 1):
            now = make(steps[i]) if i < len(steps) else None
            if held is not None:
                use(steps[i - 1], held)
            held = now

    acc[...] = jnp.zeros_like(acc)

    def make1(at):
        hot = one_hot(sender(at) - cells, 2 * reach1)
        return second_layer(1, pre3[:, at] + dot(sent[:, cells:ext], hot))

    def use1(at, v):
        acc[...] += dot_nt(normed(v).astype(BF), one_hot(recv1[at].reshape(1, w) - me * nodes, nodes))

    pipelined(steps1, make1, use1)
    ml[...] = (acc[...] * cols[:, 9:10]).astype(BF)
    copies["p00"].wait()
    link = dot_nt(ml[...].astype(F32).T.astype(BF), w_p[0, 0]).astype(BF)
    pl.semaphore_wait(stage.at[2], 3)

    def out_copy(g, k):
        dz, dy = k // 4, k % 4
        to_s = (x + g // 2 + dz + dy) % 4 * 2 + (core + g) % 2
        to_c = (z + dz) % 4 * 4 + (y + dy) % 4
        at = pl.ds(pl.multiple_of((g * 16 + k) * 16, 16), 16)
        return pltpu.make_async_remote_copy(
            outgoing.at[at],
            arrived.at[at],
            a2a_send,
            a2a_recv.at[g],
            device_id=(to_s, to_c),
            device_id_type=MESH,
        )

    order = list(range(1, 8)) + [0]
    for g in order:
        at = slice(g * 256, (g + 1) * 256)
        outgoing[at, :] = dot_tn(one_hot(rows[:, at], nodes), link).astype(BF)

        @pl.loop(0 if g else 1, 16)
        def _(k):
            out_copy(g, k).start()

    arrived[0:16, :] = outgoing[0:16, :]

    copies["p01"].wait()
    own_link = jnp.concatenate(
        [dot(w_p[0, 1], ml[...]).astype(BF), edge_columns(vec, gwt[1], fb[2:3, :])], axis=1
    )

    @pl.loop(0, edges2 // w)
    def _(i):
        at = pl.ds(pl.multiple_of(i * w, w), w)
        hot = one_hot(recv2[at].reshape(1, w) - me * nodes, nodes)
        pre[:, at] = dot(own_link, jnp.concatenate([hot, padded(features(geom2[:, at]))], axis=0))

    copies["p21"].wait()
    copies["p30"].wait()
    outp[...] = dot(w_p[3, 0], lat[...]) + cols[:, 5:6]
    both3 = jnp.concatenate([w_p[2, 1], edge_columns(vec, gwt[2], fb[4:5, :])], axis=1)

    v = send3[...].reshape(1, 3 * cells) - me * nodes
    v = jnp.where(v < 0, v + near3, v)
    feat[...] = features(geom3[...], [(v // 16).astype(F32), (v % 16).astype(F32)])
    wq = 256
    for q in range(cells // wq):
        part = feat[:, q * 3 * wq : (q + 1) * 3 * wq].astype(BF)
        here = lat[:, q * wq : (q + 1) * wq]
        for j in range(3):
            take = (
                lax.broadcasted_iota(jnp.int32, (3 * wq, wq), 0)
                == 3 * lax.broadcasted_iota(jnp.int32, (3 * wq, wq), 1) + j
            ).astype(BF)
            got = dot(part, take)
            at = slice((3 * q + j) * wq, (3 * q + j + 1) * wq)
            send4[:, at] = (got[8:9, :] * 16.0 + got[9:10, :]).astype(jnp.int32)
            pre3[:, at] = dot(both3, jnp.concatenate([here, padded(got[0:8, :])], axis=0))

    t = slot[...].reshape(1, edges2)
    p = t // 16
    dz, dy = (z - p // 4 % 4 + 4) % 4, (y - p % 4 + 4) % 4
    dx, dc = (x - p // 32 + 4) % 4, (core - p // 16 % 2 + 2) % 2
    place = ((((dx - dz - dy + 8) % 4 * 2 + dc) * 4 + dz) * 4 + dy) * 16 + t % 16

    def landed(g):
        got = arrived.at[pl.ds(0, 16 * (16 if g else 15))]
        pltpu.make_async_copy(got, got, a2a_recv.at[g]).wait()

    for pair_of in ((1, 2), (3, 4), (5, 6), (7, 0)):
        block, local = [], []
        for g in pair_of:
            landed(g)
            block.append(arrived[g * 256 : (g + 1) * 256, :])
            local.append(g * 256)
        block = jnp.concatenate(block, axis=0)
        for at in steps2:
            hot = jnp.concatenate([one_hot(place[:, at] - first, 256) for first in local], axis=0)
            pre[:, at] += dot_tn(block, hot)
    gone = outgoing.at[pl.ds(0, 16 * 127)]
    pltpu.make_async_copy(gone, gone, a2a_send).wait()

    acc[...] = jnp.zeros_like(acc)
    copies["s2"].wait()

    def use2(at, v):
        acc[...] += dot_nt(normed(v).astype(BF), one_hot(recv2[at].reshape(1, w) - me * nodes, nodes))

    pipelined(steps2, lambda at: second_layer(2, pre[:, at]), use2)

    for name in ("p10", "p11", "s3", "p20"):
        copies[name].wait()

    def update(latent, total):
        aggregate = (total * cols[:, 10:11]).astype(BF)
        hidden = silu(dot(w_p[1, 0], latent) + dot(w_p[1, 1], aggregate) + cols[:, 3:4]).astype(BF)
        state = (latent.astype(F32) + normed(dot(w_s[3], hidden)) * cols[:, 11:12]).astype(BF)
        return state, dot(w_p[2, 0], state).astype(BF)

    last = nodes - reach3
    both = lambda ref: jnp.concatenate([ref[:, 0:reach3], ref[:, last:]], axis=1)
    state, out = update(both(ml), both(acc))
    state_out[:, 0:reach3] = state[:, 0:reach3]
    state_out[:, last:] = state[:, reach3:]
    ds[:, 0:reach3] = out[:, 0:reach3]
    ds[:, last:nodes] = out[:, reach3:]
    to_right = pltpu.make_async_remote_copy(
        ds.at[:, last:nodes],
        ds.at[:, nodes + reach3 :],
        halo_send.at[2],
        halo_recv.at[2],
        device_id=right,
        device_id_type=MESH,
    )
    to_left = pltpu.make_async_remote_copy(
        ds.at[:, 0:reach3],
        ds.at[:, nodes : nodes + reach3],
        halo_send.at[3],
        halo_recv.at[3],
        device_id=left,
        device_id_type=MESH,
    )
    to_right.start()
    to_left.start()
    state, out = update(ml[:, reach3:last], acc[:, reach3:last])
    state_out[:, reach3:last] = state
    ds[:, reach3:last] = out
    save_state = pltpu.make_async_copy(state_out, state_hbm, out_sem.at[0])
    save_state.start()

    @pl.loop(0, 3 * cells // w)
    def _(i):
        at = pl.ds(pl.multiple_of(i * w, w), w)
        pre3[:, at] += dot(ds[:, 0:nodes], one_hot(send4[:, at], nodes))

    for name in ("s4", "p31", "ow"):
        copies[name].wait()
    to_right.wait()
    to_left.wait()

    outs = ow.shape[0]
    sums = {}

    def make3(step):
        q, j = step
        at = slice((3 * q + j) * wq, (3 * q + j + 1) * wq)
        hot = one_hot(send4[:, at] - nodes, 2 * reach3)
        return second_layer(4, pre3[:, at] + dot(ds[:, nodes:], hot))

    def use3(step, v):
        q, j = step
        message = normed(v).astype(BF).astype(F32)
        sums[q] = sums[q] + message if j else message
        if j == 2:
            at = slice(q * wq, (q + 1) * wq)
            gathered = (sums.pop(q) * cols[:, 12:13]).astype(BF)
            hidden = silu(outp[:, at] + dot(w_p[3, 1], gathered)).astype(BF)
            pred_out[:, at] = dot(w_o[...], hidden) + cols[0:outs, 16:17]

    pipelined([(q, j) for q in range(cells // wq) for j in range(3)], make3, use3)
    save = pltpu.make_async_copy(pred_out, pred_hbm, out_sem.at[1])
    save.start()
    save_state.wait()
    save.wait()


def keep(a, b, a_out, b_out):
    a_out[...] = a[...]
    b_out[...] = b[...]


def body(
    grid_in,
    grid_embed_w,
    g2m_w,
    pair_w,
    second_w,
    first_b,
    norm_gain,
    geom_w,
    out_w,
    out_b,
    g2m_geom,
    mesh_geom,
    m2g_geom,
    g2m_send,
    g2m_recv,
    mesh_recv,
    mesh_slot,
    mesh_rows,
    m2g_send,
):
    width, channels = grid_embed_w.shape
    cells = grid_in.shape[1]
    nodes = 512
    links = mesh_rows.size
    reach = cells // 4
    ext = cells + 2 * reach
    outs = out_w.shape[0]
    args = (
        grid_in,
        grid_embed_w.T,
        g2m_w,
        pair_w,
        second_w,
        first_b,
        norm_gain,
        geom_w.transpose(0, 2, 1),
        out_w,
        out_b.reshape(1, -1),
        g2m_geom,
        mesh_geom,
        m2g_geom,
        g2m_send,
        g2m_recv,
        mesh_recv,
        mesh_slot,
        mesh_rows.T,
        m2g_send,
    )
    hbm, vmem = pl.BlockSpec(memory_space=pl.ANY), pl.BlockSpec(memory_space=pltpu.VMEM)
    in_specs = [vmem] * len(args)
    for k in (0, 1, 2, 3, 4, 8):
        in_specs[k] = hbm
    V = pltpu.VMEM
    shapes = [jax.ShapeDtypeStruct((outs, cells), F32), jax.ShapeDtypeStruct((width, nodes), BF)]
    made = pl.pallas_call(
        kernel,
        in_specs=in_specs,
        out_specs=[hbm, hbm],
        out_shape=shapes,
        scratch_shapes=[
            V((channels, width), BF),
            V((width, width), BF),
            V(pair_w.shape, BF),
            V(second_w.shape, BF),
            V(out_w.shape, BF),
            V((channels, cells), BF),
            V((channels, reach), BF),
            V((channels, reach), BF),
            V((256, ext), BF),
            V((256, width), BF),
            V((256, width), F32),
            V((width, 128), F32),
            V((16, m2g_send.shape[0]), F32),
            V((width, ext + 256), BF),
            V((width, cells), BF),
            V((width, cells), F32),
            V((width, nodes), F32),
            V((width, nodes), BF),
            V((links, width), BF),
            V((links, width), BF),
            V((width, mesh_slot.shape[0]), F32),
            V((width, m2g_send.shape[0]), F32),
            V((width, nodes + nodes // 2), BF),
            V((1, m2g_send.shape[0]), jnp.int32),
            V((outs, cells), F32),
            V((width, nodes), BF),
            pltpu.SemaphoreType.DMA((17,)),
            pltpu.SemaphoreType.DMA((4,)),
            pltpu.SemaphoreType.DMA((4,)),
            pltpu.SemaphoreType.DMA,
            pltpu.SemaphoreType.DMA((8,)),
            pltpu.SemaphoreType.DMA((2,)),
            pltpu.SemaphoreType.REGULAR((3,)),
        ],
        compiler_params=pltpu.CompilerParams(
            collective_id=0, has_side_effects=True, vmem_limit_bytes=60 << 20
        ),
        name="graph",
    )(*args)
    blocks = [pl.BlockSpec((outs, cells // 4), lambda i: (0, i)), pl.BlockSpec((width // 4, nodes), lambda i: (i, 0))]
    return tuple(
        pl.pallas_call(
            keep,
            grid=(4,),
            in_specs=blocks,
            out_specs=blocks,
            out_shape=shapes,
            name="keep",
        )(*made)
    )


def solution(mesh):
    return jax.shard_map(
        body,
        mesh=mesh,
        in_specs=(
            P(None, AXES),
            P(),
            P(),
            P(),
            P(),
            P(),
            P(),
            P(),
            P(),
            P(),
            P(None, AXES),
            P(None, AXES),
            P(None, AXES),
            P(AXES),
            P(AXES),
            P(AXES),
            P(AXES),
            P(AXES, None),
            P(AXES),
        ),
        out_specs=(P(None, AXES), P(None, AXES)),
        check_vma=False,
    )
```

time: 82.6 us -> 72.4 us (0.88)
  the two profiles are of different devices: /device:TPU:0 before, /device:TPU:1 now
where the time goes in v3:
time: 72.4 us; the launch traced here: 72.2 us
  Pallas kernels  71.6 us (99%)
    pallas_call x1, Pallas kernels, body(): pl.pallas_call(kernel, in_specs=in_specs, out_specs=[hbm, hbm], out_shape...  67.9 us
    pallas_call x1, Pallas kernels, body(): pl.pallas_call(keep, grid=(4,), in_specs=blocks, out_specs=blocks, out_sh...  3.61 us

profile of v3, /device:TPU:1, one launch (start us, length us, event | category | flops | bytes accessed | tf_op | source)
XLA Modules:
  0.0 72.2 jit_solution(14210242280322238725)
XLA Ops:
  0.6 67.9 %graph.1 = (f32[227,1024]{1,0:T(8,128)}, bf16[512,512]{1,0:T(8,128)(2,1)}) custom-call(bf16[227,1024]{1,0:T(8,128)(2,1)} %gin.1, bf16[227,512]{1,0:T(8,128)(2,1)} %bitcast.4, bf16[512,512]{1,0:T(8,128)(2,1)} %g2m.1, bf16[4,2,512,512]{3,2,1,0:T(8,128)(2,1)} %pair.1, bf16[5,512,512]{2,1,0:T(8,128)(2,1)} %second.1, f32[6,512]{1,0:T(8,128)} %fb.1, f32[5,512]{1,0:T(8,128)} %ng.1, ...), custom_call_target="tpu_custom_call" | custom-call | tf_op jit(solution)/shard_map/graph/pallas_call | solution.py:499
  68.6 3.6 %keep.1 = (f32[227,1024]{1,0:T(8,128)}, bf16[512,512]{1,0:T(8,128)(2,1)}) custom-call(f32[227,1024]{1,0:T(8,128)} %get-tuple-element.4.a, bf16[512,512]{1,0:T(8,128)(2,1)} %get-tuple-element.5.b), custom_call_target="tpu_custom_call" | custom-call | tf_op jit(solution)/shard_map/keep/pallas_call | solution.py:546

commit v4 on v3

--- a/solution.py
+++ b/solution.py
@@ -101,6 +101,7 @@
     sent,
     lat,
     outp,
+    node,
     acc,
     ml,
     outgoing,
@@ -108,6 +109,10 @@
     pre,
     pre3,
     ds,
+    first_out,
+    last_out,
+    next_in,
+    prev_in,
     send4,
     pred_out,
     state_out,
@@ -186,13 +191,14 @@
     vec[8:13, :] = ng[...]
     vec[16:17, 0 : ob.shape[1]] = ob[...]
     cols[...] = vec[0:128, :].T
-    embed[...] = jnp.zeros_like(embed)
-    ginx[...] = jnp.zeros_like(ginx)
+    channels = own.shape[0]
+    pad = channels // 16 * 16
+    embed[pad:, :] = jnp.zeros((embed.shape[0] - pad, width), BF)
+    ginx[pad:, :] = jnp.zeros((embed.shape[0] - pad, ext), BF)
     sent[:, ext:] = edge_columns(vec, gwt[0], fb[1:2, :])
 
     copies["we"].wait()
     copies["own"].wait()
-    channels = own.shape[0]
     embed[0:channels, :] = w_e[...]
 
     def embedded(values):
@@ -239,7 +245,12 @@
     to_left.wait()
     ginx[0:channels, cells : cells + reach1] = high[...]
     ginx[0:channels, cells + reach1 :] = low[...]
-    sent[:, cells:ext] = dot(w_g[...], embedded(ginx[:, cells:])).astype(BF)
+    halves = [slice(cells, cells + reach1), slice(cells + reach1, ext)]
+    values = [dot_tn(embed[...], ginx[:, at]) + cols[:, 0:1] for at in halves]
+    values = [dot(w_s[0], silu(v).astype(BF)) for v in values]
+    values = [(normed(v) * cols[:, 8:9]).astype(BF) for v in values]
+    for at, v in zip(halves, values):
+        sent[:, at] = dot(w_g[...], v).astype(BF)
     pl.semaphore_wait(stage.at[1], 3)
     meet(2, x_peers)
 
@@ -307,8 +318,9 @@
         hot = one_hot(recv2[at].reshape(1, w) - me * nodes, nodes)
         pre[:, at] = dot(own_link, jnp.concatenate([hot, padded(features(geom2[:, at]))], axis=0))
 
-    copies["p21"].wait()
-    copies["p30"].wait()
+    for name in ("p21", "p30", "p10"):
+        copies[name].wait()
+    node[...] = dot(w_p[1, 0], ml[...]) + cols[:, 3:4]
     outp[...] = dot(w_p[3, 0], lat[...]) + cols[:, 5:6]
     both3 = jnp.concatenate([w_p[2, 1], edge_columns(vec, gwt[2], fb[4:5, :])], axis=1)
 
@@ -360,50 +372,44 @@
 
     pipelined(steps2, lambda at: second_layer(2, pre[:, at]), use2)
 
-    for name in ("p10", "p11", "s3", "p20"):
+    for name in ("p11", "s3", "p20"):
         copies[name].wait()
-
-    def update(latent, total):
-        aggregate = (total * cols[:, 10:11]).astype(BF)
-        hidden = silu(dot(w_p[1, 0], latent) + dot(w_p[1, 1], aggregate) + cols[:, 3:4]).astype(BF)
-        state = (latent.astype(F32) + normed(dot(w_s[3], hidden)) * cols[:, 11:12]).astype(BF)
-        return state, dot(w_p[2, 0], state).astype(BF)
 
     last = nodes - reach3
     both = lambda ref: jnp.concatenate([ref[:, 0:reach3], ref[:, last:]], axis=1)
-    state, out = update(both(ml), both(acc))
+    middle = lambda ref: ref[:, reach3:last]
+    values = [pick(node) + dot(w_p[1, 1], (pick(acc) * cols[:, 10:11]).astype(BF)) for pick in (both, middle)]
+    values = [dot(w_s[3], silu(v).astype(BF)) for v in values]
+
+    def states(pick, v):
+        return (pick(ml).astype(F32) + normed(v) * cols[:, 11:12]).astype(BF)
+
+    state = states(both, values[0])
+    out = dot(w_p[2, 0], state).astype(BF)
+    first_out[...] = out[:, 0:reach3]
+    last_out[...] = out[:, reach3:]
+    to_right = pltpu.make_async_remote_copy(
+        last_out, prev_in, halo_send.at[2], halo_recv.at[2], device_id=right, device_id_type=MESH
+    )
+    to_left = pltpu.make_async_remote_copy(
+        first_out, next_in, halo_send.at[3], halo_recv.at[3], device_id=left, device_id_type=MESH
+    )
+    to_right.start()
+    to_left.start()
     state_out[:, 0:reach3] = state[:, 0:reach3]
     state_out[:, last:] = state[:, reach3:]
     ds[:, 0:reach3] = out[:, 0:reach3]
-    ds[:, last:nodes] = out[:, reach3:]
-    to_right = pltpu.make_async_remote_copy(
-        ds.at[:, last:nodes],
-        ds.at[:, nodes + reach3 :],
-        halo_send.at[2],
-        halo_recv.at[2],
-        device_id=right,
-        device_id_type=MESH,
-    )
-    to_left = pltpu.make_async_remote_copy(
-        ds.at[:, 0:reach3],
-        ds.at[:, nodes : nodes + reach3],
-        halo_send.at[3],
-        halo_recv.at[3],
-        device_id=left,
-        device_id_type=MESH,
-    )
-    to_right.start()
-    to_left.start()
-    state, out = update(ml[:, reach3:last], acc[:, reach3:last])
+    ds[:, last:] = out[:, reach3:]
+    state = states(middle, values[1])
     state_out[:, reach3:last] = state
-    ds[:, reach3:last] = out
+    ds[:, reach3:last] = dot(w_p[2, 0], state).astype(BF)
     save_state = pltpu.make_async_copy(state_out, state_hbm, out_sem.at[0])
     save_state.start()
 
     @pl.loop(0, 3 * cells // w)
     def _(i):
         at = pl.ds(pl.multiple_of(i * w, w), w)
-        pre3[:, at] += dot(ds[:, 0:nodes], one_hot(send4[:, at], nodes))
+        pre3[:, at] += dot(ds[...], one_hot(send4[:, at], nodes))
 
     for name in ("s4", "p31", "ow"):
         copies[name].wait()
@@ -411,13 +417,14 @@
     to_left.wait()
 
     outs = ow.shape[0]
-    sums = {}
+    near = jnp.concatenate([next_in[...], prev_in[...]], axis=1)
+    sums, saves = {}, []
 
     def make3(step):
         q, j = step
         at = slice((3 * q + j) * wq, (3 * q + j + 1) * wq)
         hot = one_hot(send4[:, at] - nodes, 2 * reach3)
-        return second_layer(4, pre3[:, at] + dot(ds[:, nodes:], hot))
+        return second_layer(4, pre3[:, at] + dot(near, hot))
 
     def use3(step, v):
         q, j = step
@@ -428,12 +435,12 @@
             gathered = (sums.pop(q) * cols[:, 12:13]).astype(BF)
             hidden = silu(outp[:, at] + dot(w_p[3, 1], gathered)).astype(BF)
             pred_out[:, at] = dot(w_o[...], hidden) + cols[0:outs, 16:17]
+            saves.append(pltpu.make_async_copy(pred_out.at[:, at], pred_hbm.at[:, at], out_sem.at[1 + q]))
+            saves[-1].start()
 
     pipelined([(q, j) for q in range(cells // wq) for j in range(3)], make3, use3)
-    save = pltpu.make_async_copy(pred_out, pred_hbm, out_sem.at[1])
-    save.start()
-    save_state.wait()
-    save.wait()
+    for save in [save_state] + saves:
+        save.wait()
 
 
 def keep(a, b, a_out, b_out):
@@ -519,12 +526,17 @@
             V((width, cells), BF),
             V((width, cells), F32),
             V((width, nodes), F32),
+            V((width, nodes), F32),
             V((width, nodes), BF),
             V((links, width), BF),
             V((links, width), BF),
             V((width, mesh_slot.shape[0]), F32),
             V((width, m2g_send.shape[0]), F32),
-            V((width, nodes + nodes // 2), BF),
+            V((width, nodes), BF),
+            V((width, nodes // 4), BF),
+            V((width, nodes // 4), BF),
+            V((width, nodes // 4), BF),
+            V((width, nodes // 4), BF),
             V((1, m2g_send.shape[0]), jnp.int32),
             V((outs, cells), F32),
             V((width, nodes), BF),
@@ -533,7 +545,7 @@
             pltpu.SemaphoreType.DMA((4,)),
             pltpu.SemaphoreType.DMA,
             pltpu.SemaphoreType.DMA((8,)),
-            pltpu.SemaphoreType.DMA((2,)),
+            pltpu.SemaphoreType.DMA((1 + cells // 256,)),
             pltpu.SemaphoreType.REGULAR((3,)),
         ],
         compiler_params=pltpu.CompilerParams(
@@ -541,11 +553,11 @@
         ),
         name="graph",
     )(*args)
-    blocks = [pl.BlockSpec((outs, cells // 4), lambda i: (0, i)), pl.BlockSpec((width // 4, nodes), lambda i: (i, 0))]
+    blocks = [pl.BlockSpec((outs, cells // 2), lambda i: (0, i)), pl.BlockSpec((width // 2, nodes), lambda i: (i, 0))]
     return tuple(
         pl.pallas_call(
             keep,
-            grid=(4,),
+            grid=(2,),
             in_specs=blocks,
             out_specs=blocks,
             out_shape=shapes,

time: 72.4 us -> 70.6 us (0.975)
  Pallas kernels: 71.6 us -> 69.8 us
    pallas_call x1, Pallas kernels: 3.61 us -> 2.26 us  [body(): pl.pallas_call(keep, grid=(2,), in_specs=blocks, out_specs=blocks, out_sh...]
where the time goes in v4:
time: 70.6 us; the launch traced here: 70.4 us
  Pallas kernels  69.8 us (99%)
    pallas_call x1, Pallas kernels, body(): pl.pallas_call(kernel, in_specs=in_specs, out_specs=[hbm, hbm], out_shape...  67.5 us
    pallas_call x1, Pallas kernels, body(): pl.pallas_call(keep, grid=(2,), in_specs=blocks, out_specs=blocks, out_sh...  2.26 us

profile of v4, /device:TPU:1, one launch (start us, length us, event | category | flops | bytes accessed | tf_op | source)
XLA Modules:
  0.0 70.4 jit_solution(14461626207390826690)
XLA Ops:
  0.6 67.5 %graph.1 = (f32[227,1024]{1,0:T(8,128)}, bf16[512,512]{1,0:T(8,128)(2,1)}) custom-call(bf16[227,1024]{1,0:T(8,128)(2,1)} %gin.1, bf16[227,512]{1,0:T(8,128)(2,1)} %bitcast.4, bf16[512,512]{1,0:T(8,128)(2,1)} %g2m.1, bf16[4,2,512,512]{3,2,1,0:T(8,128)(2,1)} %pair.1, bf16[5,512,512]{2,1,0:T(8,128)(2,1)} %second.1, f32[6,512]{1,0:T(8,128)} %fb.1, f32[5,512]{1,0:T(8,128)} %ng.1, ...), custom_call_target="tpu_custom_call" | custom-call | tf_op jit(solution)/shard_map/graph/pallas_call | solution.py:506
  68.2 2.3 %keep.1 = (f32[227,1024]{1,0:T(8,128)}, bf16[512,512]{1,0:T(8,128)(2,1)}) custom-call(f32[227,1024]{1,0:T(8,128)} %get-tuple-element.4.a, bf16[512,512]{1,0:T(8,128)(2,1)} %get-tuple-element.5.b), custom_call_target="tpu_custom_call" | custom-call | tf_op jit(solution)/shard_map/keep/pallas_call | solution.py:558

commit v5 on v4

--- a/solution.py
+++ b/solution.py
@@ -69,20 +69,20 @@
     g2m,
     pair,
     second,
-    fb,
-    ng,
-    gwt,
+    fb_hbm,
+    ng_hbm,
+    gwt_hbm,
     ow,
-    ob,
-    geom1,
-    geom2,
-    geom3,
-    send1,
-    recv1,
-    recv2,
-    slot,
-    rows_t,
-    send3,
+    ob_hbm,
+    geom1_hbm,
+    geom2_hbm,
+    geom3_hbm,
+    send1_hbm,
+    recv1_hbm,
+    recv2_hbm,
+    slot_hbm,
+    rows_t_hbm,
+    send3_hbm,
     pred_hbm,
     state_hbm,
     w_e,
@@ -103,6 +103,8 @@
     outp,
     node,
     acc,
+    ends,
+    message,
     ml,
     outgoing,
     arrived,
@@ -123,6 +125,19 @@
     a2a_recv,
     out_sem,
     stage,
+    fb,
+    ng,
+    gwt,
+    ob,
+    geom1,
+    geom2,
+    geom3,
+    send1,
+    recv1,
+    recv2,
+    slot,
+    rows_t,
+    send3,
 ):
     s, c = lax.axis_index("space"), lax.axis_index("chan")
     me = s * 16 + c
@@ -157,6 +172,23 @@
         copies[name] = pltpu.make_async_copy(src, dst, w_sem.at[len(copies)])
         copies[name].start()
 
+    smalls = (
+        ("fb", fb_hbm, fb),
+        ("ng", ng_hbm, ng),
+        ("gwt", gwt_hbm, gwt),
+        ("ob", ob_hbm, ob),
+        ("geom1", geom1_hbm, geom1),
+        ("geom2", geom2_hbm, geom2),
+        ("geom3", geom3_hbm, geom3),
+        ("send1", send1_hbm, send1),
+        ("recv1", recv1_hbm, recv1),
+        ("recv2", recv2_hbm, recv2),
+        ("slot", slot_hbm, slot),
+        ("rows_t", rows_t_hbm, rows_t),
+        ("send3", send3_hbm, send3),
+    )
+    for small in smalls:
+        fetch(*small)
     fetch("own", gin, own)
     fetch("we", wet, w_e)
     fetch("s0", second.at[0], w_s.at[0])
@@ -186,6 +218,9 @@
     to_left.start()
     meet(0, y_peers)
 
+    for small in smalls:
+        copies[small[0]].wait()
+
     vec[...] = jnp.zeros_like(vec)
     vec[0:6, :] = fb[...]
     vec[8:13, :] = ng[...]
@@ -351,9 +386,9 @@
         got = arrived.at[pl.ds(0, 16 * (16 if g else 15))]
         pltpu.make_async_copy(got, got, a2a_recv.at[g]).wait()
 
-    for pair_of in ((1, 2), (3, 4), (5, 6), (7, 0)):
+    for group in ((1, 2), (3, 4), (5, 6), (7,)):
         block, local = [], []
-        for g in pair_of:
+        for g in group:
             landed(g)
             block.append(arrived[g * 256 : (g + 1) * 256, :])
             local.append(g * 256)
@@ -361,31 +396,41 @@
         for at in steps2:
             hot = jnp.concatenate([one_hot(place[:, at] - first, 256) for first in local], axis=0)
             pre[:, at] += dot_tn(block, hot)
+    copies["s2"].wait()
+    landed(0)
     gone = outgoing.at[pl.ds(0, 16 * 127)]
     pltpu.make_async_copy(gone, gone, a2a_send).wait()
 
-    acc[...] = jnp.zeros_like(acc)
-    copies["s2"].wait()
+    last = nodes - reach3
+    ends[...] = jnp.zeros_like(ends)
+
+    def receiver(at):
+        return recv2[at].reshape(1, -1) - me * nodes
+
+    def make2(at):
+        return second_layer(2, pre[:, at] + dot_tn(arrived[0:256, :], one_hot(place[:, at], 256)))
 
     def use2(at, v):
-        acc[...] += dot_nt(normed(v).astype(BF), one_hot(recv2[at].reshape(1, w) - me * nodes, nodes))
-
-    pipelined(steps2, lambda at: second_layer(2, pre[:, at]), use2)
+        message[:, at] = normed(v).astype(BF)
+        to = receiver(at)
+        to = jnp.where(to < reach3, to, jnp.where(to < last, -1, to - (nodes - 2 * reach3)))
+        ends[...] += dot_nt(message[:, at], one_hot(to, 2 * reach3))
+
+    pipelined(steps2, make2, use2)
 
     for name in ("p11", "s3", "p20"):
         copies[name].wait()
 
-    last = nodes - reach3
     both = lambda ref: jnp.concatenate([ref[:, 0:reach3], ref[:, last:]], axis=1)
     middle = lambda ref: ref[:, reach3:last]
-    values = [pick(node) + dot(w_p[1, 1], (pick(acc) * cols[:, 10:11]).astype(BF)) for pick in (both, middle)]
-    values = [dot(w_s[3], silu(v).astype(BF)) for v in values]
-
-    def states(pick, v):
-        return (pick(ml).astype(F32) + normed(v) * cols[:, 11:12]).astype(BF)
-
-    state = states(both, values[0])
-    out = dot(w_p[2, 0], state).astype(BF)
+
+    def update(pick, total):
+        v = pick(node) + dot(w_p[1, 1], (total * cols[:, 10:11]).astype(BF))
+        v = normed(dot(w_s[3], silu(v).astype(BF)))
+        state = (pick(ml).astype(F32) + v * cols[:, 11:12]).astype(BF)
+        return state, dot(w_p[2, 0], state).astype(BF)
+
+    state, out = update(both, ends[...])
     first_out[...] = out[:, 0:reach3]
     last_out[...] = out[:, reach3:]
     to_right = pltpu.make_async_remote_copy(
@@ -400,9 +445,10 @@
     state_out[:, last:] = state[:, reach3:]
     ds[:, 0:reach3] = out[:, 0:reach3]
     ds[:, last:] = out[:, reach3:]
-    state = states(middle, values[1])
+    total = dot_nt(message[...], one_hot(receiver(slice(0, edges2)) - reach3, last - reach3))
+    state, out = update(middle, total)
     state_out[:, reach3:last] = state
-    ds[:, reach3:last] = dot(w_p[2, 0], state).astype(BF)
+    ds[:, reach3:last] = out
     save_state = pltpu.make_async_copy(state_out, state_hbm, out_sem.at[0])
     save_state.start()
 
@@ -428,8 +474,8 @@
 
     def use3(step, v):
         q, j = step
-        message = normed(v).astype(BF).astype(F32)
-        sums[q] = sums[q] + message if j else message
+        v = normed(v).astype(BF).astype(F32)
+        sums[q] = sums[q] + v if j else v
         if j == 2:
             at = slice(q * wq, (q + 1) * wq)
             gathered = (sums.pop(q) * cols[:, 12:13]).astype(BF)
@@ -497,15 +543,12 @@
         mesh_rows.T,
         m2g_send,
     )
-    hbm, vmem = pl.BlockSpec(memory_space=pl.ANY), pl.BlockSpec(memory_space=pltpu.VMEM)
-    in_specs = [vmem] * len(args)
-    for k in (0, 1, 2, 3, 4, 8):
-        in_specs[k] = hbm
+    hbm = pl.BlockSpec(memory_space=pl.ANY)
     V = pltpu.VMEM
     shapes = [jax.ShapeDtypeStruct((outs, cells), F32), jax.ShapeDtypeStruct((width, nodes), BF)]
     made = pl.pallas_call(
         kernel,
-        in_specs=in_specs,
+        in_specs=[hbm] * len(args),
         out_specs=[hbm, hbm],
         out_shape=shapes,
         scratch_shapes=[
@@ -527,6 +570,8 @@
             V((width, cells), F32),
             V((width, nodes), F32),
             V((width, nodes), F32),
+            V((width, nodes // 2), F32),
+            V((width, mesh_slot.shape[0]), BF),
             V((width, nodes), BF),
             V((links, width), BF),
             V((links, width), BF),
@@ -540,14 +585,15 @@
             V((1, m2g_send.shape[0]), jnp.int32),
             V((outs, cells), F32),
             V((width, nodes), BF),
-            pltpu.SemaphoreType.DMA((17,)),
+            pltpu.SemaphoreType.DMA((30,)),
             pltpu.SemaphoreType.DMA((4,)),
             pltpu.SemaphoreType.DMA((4,)),
             pltpu.SemaphoreType.DMA,
             pltpu.SemaphoreType.DMA((8,)),
             pltpu.SemaphoreType.DMA((1 + cells // 256,)),
             pltpu.SemaphoreType.REGULAR((3,)),
-        ],
+        ]
+        + [V(a.shape, a.dtype) for a in args[5:8] + args[9:]],
         compiler_params=pltpu.CompilerParams(
             collective_id=0, has_side_effects=True, vmem_limit_bytes=60 << 20
         ),

time: 70.6 us -> 69 us (0.977)
  Pallas kernels: 69.8 us -> 68.2 us
    pallas_call x1, Pallas kernels: 67.5 us -> 66 us  [body(): pl.pallas_call(kernel, in_specs=[hbm] * len(args), out_specs=[hbm, hbm],...]
where the time goes in v5:
time: 69 us; the launch traced here: 68.9 us
  Pallas kernels  68.2 us (99%)
    pallas_call x1, Pallas kernels, body(): pl.pallas_call(kernel, in_specs=[hbm] * len(args), out_specs=[hbm, hbm],...  66 us
    pallas_call x1, Pallas kernels, body(): pl.pallas_call(keep, grid=(2,), in_specs=blocks, out_specs=blocks, out_sh...  2.26 us

profile of v5, /device:TPU:1, one launch (start us, length us, event | category | flops | bytes accessed | tf_op | source)
XLA Modules:
  0.0 68.9 jit_solution(11675843862475260302)
XLA Ops:
  0.6 66.0 %graph.1 = (f32[227,1024]{1,0:T(8,128)}, bf16[512,512]{1,0:T(8,128)(2,1)}) custom-call(bf16[227,1024]{1,0:T(8,128)(2,1)} %gin.1, bf16[227,512]{1,0:T(8,128)(2,1)} %bitcast.4, bf16[512,512]{1,0:T(8,128)(2,1)} %g2m.1, bf16[4,2,512,512]{3,2,1,0:T(8,128)(2,1)} %pair.1, bf16[5,512,512]{2,1,0:T(8,128)(2,1)} %second.1, f32[6,512]{1,0:T(8,128)} %fb_hbm.1, ...), custom_call_target="tpu_custom_call" | custom-call | tf_op jit(solution)/shard_map/graph/pallas_call | solution.py:549
  66.6 2.3 %keep.1 = (f32[227,1024]{1,0:T(8,128)}, bf16[512,512]{1,0:T(8,128)(2,1)}) custom-call(f32[227,1024]{1,0:T(8,128)} %get-tuple-element.4.a, bf16[512,512]{1,0:T(8,128)(2,1)} %get-tuple-element.5.b), custom_call_target="tpu_custom_call" | custom-call | tf_op jit(solution)/shard_map/keep/pallas_call | solution.py:604

commit v6 on v5

--- a/solution.py
+++ b/solution.py
@@ -452,9 +452,9 @@
     save_state = pltpu.make_async_copy(state_out, state_hbm, out_sem.at[0])
     save_state.start()
 
-    @pl.loop(0, 3 * cells // w)
+    @pl.loop(0, 3)
     def _(i):
-        at = pl.ds(pl.multiple_of(i * w, w), w)
+        at = pl.ds(pl.multiple_of(i * cells, cells), cells)
         pre3[:, at] += dot(ds[...], one_hot(send4[:, at], nodes))
 
     for name in ("s4", "p31", "ow"):

time: 69 us -> 69 us (level)
  no operation moved by 1% of the time
where the time goes in v6:
time: 69 us; the launch traced here: 68.9 us
  Pallas kernels  68.2 us (99%)
    pallas_call x1, Pallas kernels, body(): pl.pallas_call(kernel, in_specs=[hbm] * len(args), out_specs=[hbm, hbm],...  66 us
    pallas_call x1, Pallas kernels, body(): pl.pallas_call(keep, grid=(2,), in_specs=blocks, out_specs=blocks, out_sh...  2.26 us

profile of v6, /device:TPU:1, one launch (start us, length us, event | category | flops | bytes accessed | tf_op | source)
XLA Modules:
  0.0 68.9 jit_solution(6737152542605577477)
XLA Ops:
  0.6 66.0 %graph.1 = (f32[227,1024]{1,0:T(8,128)}, bf16[512,512]{1,0:T(8,128)(2,1)}) custom-call(bf16[227,1024]{1,0:T(8,128)(2,1)} %gin.1, bf16[227,512]{1,0:T(8,128)(2,1)} %bitcast.4, bf16[512,512]{1,0:T(8,128)(2,1)} %g2m.1, bf16[4,2,512,512]{3,2,1,0:T(8,128)(2,1)} %pair.1, bf16[5,512,512]{2,1,0:T(8,128)(2,1)} %second.1, f32[6,512]{1,0:T(8,128)} %fb_hbm.1, ...), custom_call_target="tpu_custom_call" | custom-call | tf_op jit(solution)/shard_map/graph/pallas_call | solution.py:549
  66.6 2.3 %keep.1 = (f32[227,1024]{1,0:T(8,128)}, bf16[512,512]{1,0:T(8,128)(2,1)}) custom-call(f32[227,1024]{1,0:T(8,128)} %get-tuple-element.4.a, bf16[512,512]{1,0:T(8,128)(2,1)} %get-tuple-element.5.b), custom_call_target="tpu_custom_call" | custom-call | tf_op jit(solution)/shard_map/keep/pallas_call | solution.py:604
